TPU v7x, 128 devices: a whole 4x4x4 slice. The times are simulated.
128 devices in a mesh: role: 2 (over y_lo), dev: 64 (over z, y_hi, x, core).
Axes of the slice: x: 4, y: 4 (y_hi: 2, y_lo: 2; y = y_hi * 2 + y_lo), z: 4, core: 2. Of those that a mesh axis runs over, the one named last changes fastest.
Arguments:
- features: bfloat16 [2, 32, 128, 64, 128], P('role', None, 'dev'), may hold values from -6 to 6
- labels: bfloat16 [2, 128, 64, 128], P('role', 'dev'), may hold values from 0 to 1
- crop_block: int32 [2, 64, 64], P('role'), may hold values from -1 to 15, as said below
- weight: float32 [64, 864], P('dev'), may hold values from -0.21875 to 0.21875
- gain: float32 [64], P('dev'), may hold values from 0.1 to 1.9
- shift: float32 [64], P('dev'), may hold values from -3 to 3
- head: float32 [64], P('dev'), may hold values from -1.5 to 1.5
- run_mean: float32 [64], P('dev'), may hold values from -2 to 2
- run_var: float32 [64], P('dev'), may hold values from 0.5 to 2
Outputs:
- scores: float32 [2, 128, 64, 128], P('role', 'dev')
- weight_grad: float32 [64, 864], P('dev')
- vector_grad: float32 [64, 3], P('dev')
Inputs may be any that keep to these rules, and one draw needn't show every extreme that they name: crop_block[g, s, t] >= 0 is the row block b that source s of group g sends to learner t; -1 means no crop. Source s always sends to learner s, and to between 16 and 48 learners in all.
All inputs are finite; a program needn't handle non-finite values.
Results may differ from a plain program's by a relative error of at most 0.002.
The roundings to bfloat16 on the way count: a program that leaves them out, or rounds other values in their place, can miss the bound.
Values may be sent and summed in bfloat16 or wider, within the bound.
No kernel may reach another device: no remote copies, remote signals or barrier semaphores. Data moves between devices by JAX's collectives and lax.ppermute only.
A program may use at most 128 MiB of HBM per device.

v0:
```python
import jax
import jax.numpy as jnp
from jax import lax
from jax.sharding import PartitionSpec as P

CY = 4


epsilon = 1e-05


def sent_together(arrays, axis, dim, along):
    both = jnp.concatenate(arrays, axis=along)
    filled, at, finished = (lax.all_gather(both, axis, axis=dim, tiled=True), 0, [])
    for a in arrays:
        finished.append(lax.slice_in_dim(filled, at, at + a.shape[along], axis=along))
        at += a.shape[along]
    return tuple(finished)


def extended(cells, sides, width):
    for axis, dim in sides:
        count = lax.axis_size(axis)
        ends = count - 1
        head = lax.slice_in_dim(cells, 0, width, axis=dim)
        tail = lax.slice_in_dim(cells, cells.shape[dim] - width, cells.shape[dim], axis=dim)
        cells = jnp.concatenate(
            [
                lax.ppermute(tail, axis, [(i, (i + 1) % count) for i in range(ends)]),
                cells,
                lax.ppermute(head, axis, [((i + 1) % count, i) for i in range(ends)]),
            ],
            axis=dim,
        )
    return cells


def in_blocks(array, dim, devices):
    before, after = (array.shape[:dim], array.shape[dim + 1 :])
    return jnp.moveaxis(array.reshape(*before, devices, -1, *after), dim, 0)


def summed_on_arrival(array, axis, dim):
    devices = lax.axis_size(axis)
    parts = lax.all_to_all(in_blocks(array, dim, devices), axis, 0, 0, tiled=True)
    return jnp.sum(parts, axis=0)


def sent_together_2(arrays, axis, dim, along):
    ends, at = ([], 0)
    for a in arrays[:-1]:
        at += a.shape[along]
        ends.append(at)
    both = jnp.concatenate(arrays, axis=along)
    return tuple(jnp.split(summed_on_arrival(both, axis, dim), ends, axis=along))


def sent_to_all(array, axis):
    devices = lax.axis_size(axis)
    return lax.all_to_all(
        jnp.broadcast_to(array[None], (devices, *array.shape)), axis, 0, 0, tiled=True
    )


def over_copies(array, axis):
    everything = sent_to_all(array, axis)
    return jnp.sum(everything, axis=0)


def in_one(arrays, axis):
    line, at, finished = (jnp.concatenate([a.reshape(-1) for a in arrays]), 0, [])
    so_far = over_copies(line, axis)
    for a in arrays:
        finished.append(so_far[at : at + a.size].reshape(a.shape))
        at += a.size
    return tuple(finished)


def column_shift(values, offset):
    if offset < 0:
        return jnp.pad(values[..., :-1], [(0, 0)] * (values.ndim - 1) + [(1, 0)])
    return jnp.pad(values[..., 1:], [(0, 0)] * (values.ndim - 1) + [(0, 1)])


def plane_patches(padded, planes, height):
    shifted = [
        padded[:, shift_z : shift_z + planes, :, shift_y : shift_y + height, :]
        for shift_z in range(3)
        for shift_y in range(3)
    ]
    return jnp.stack(shifted, 0).reshape(9 * padded.shape[0], -1)


def conv_taps(padded, weight_taps, planes, height):
    columns = padded.shape[-1]
    patches = plane_patches(padded, planes, height)
    outputs = [
        jnp.dot(weight_taps[tap], patches, preferred_element_type=jnp.float32).reshape(
            weight_taps.shape[1], -1, columns
        )
        for tap in range(3)
    ]
    summed = outputs[1] + column_shift(outputs[0], -1) + column_shift(outputs[2], 1)
    return summed.reshape(weight_taps.shape[1], -1)


def local_total(members):
    return tuple(
        (jnp.broadcast_to(jnp.sum(member, 1, keepdims=True), member.shape) for member in members)
    )


def learn(
    crop_data,
    targets,
    live_flags,
    cell_counts,
    weight_taps,
    gain_value,
    shift_value,
    head_value,
    combine,
):
    slot_group = 8
    channels, planes, slots, crop_rows, columns = crop_data.shape
    out_channels = weight_taps.shape[1]
    row_cells = crop_rows * columns
    targets = targets.reshape(planes, slots, row_cells).astype(jnp.float32)
    live_weights = live_flags.astype(jnp.float32)
    ordering = jnp.argsort(1 - live_flags.astype(jnp.int32), stable=True)
    crop_data = crop_data[:, :, ordering]
    targets = targets[:, ordering]
    live_weights = live_weights[ordering]
    cell_counts = cell_counts[ordering]
    groups = (jnp.sum(live_flags.astype(jnp.int32)) + slot_group - 1) // slot_group

    def collect_batch_statistics(members):
        spread = tuple((jnp.zeros_like(member).at[:, ordering].set(member) for member in members))
        return tuple((result[:, ordering] for result in combine(spread)))

    def select_group(array, crop_position, axis):
        return lax.dynamic_slice_in_dim(array, crop_position, slot_group, axis)

    def update_group(array, values, crop_position, axis):
        return lax.dynamic_update_slice_in_dim(array, values, crop_position, axis)

    def crop_patches(crop_position):
        group_block = select_group(crop_data, crop_position, 2)
        return jnp.pad(group_block, ((0, 0), (1, 1), (0, 0), (1, 1), (0, 0)))

    def forward(number, stored):
        crop_position = number * slot_group
        conv_out = conv_taps(crop_patches(crop_position), weight_taps, planes, crop_rows)
        conv_out = conv_out.reshape(out_channels, planes, slot_group, row_cells).astype(
            jnp.bfloat16
        )
        return update_group(stored, conv_out, crop_position, 2)

    stored = lax.fori_loop(
        0, groups, forward, jnp.zeros((out_channels, planes, slots, row_cells), jnp.bfloat16)
    )
    slot_sums = jnp.einsum(
        "cpsk,k->cs",
        stored,
        jnp.ones((row_cells,), jnp.bfloat16),
        preferred_element_type=jnp.float32,
    )
    (mean_sum,) = collect_batch_statistics((slot_sums,))
    channel_means = mean_sum / cell_counts[None, :]

    def centred(number, squares):
        crop_position = number * slot_group
        diff = (
            select_group(stored, crop_position, 2).astype(jnp.float32)
            - select_group(channel_means, crop_position, 1)[:, None, :, None]
        ) * select_group(live_weights, crop_position, 0)[None, None, :, None]
        return update_group(squares, jnp.sum(diff * diff, (1, 3)), crop_position, 1)

    empty_statistics = jnp.zeros((out_channels, slots), jnp.float32)
    squares = lax.fori_loop(0, groups, centred, empty_statistics)
    (square_sum,) = collect_batch_statistics((squares,))
    inverse_std = lax.rsqrt(square_sum / cell_counts[None, :] + epsilon)

    def local_grads(crop_position):
        normal = (
            select_group(stored, crop_position, 2).astype(jnp.float32)
            - select_group(channel_means, crop_position, 1)[:, None, :, None]
        ) * select_group(inverse_std, crop_position, 1)[:, None, :, None]
        before = gain_value[:, None, None, None] * normal + shift_value[:, None, None, None]
        hidden = jax.nn.relu(before)
        ranked_crops = jnp.einsum(
            "cpsk,c->psk", hidden, head_value, precision=lax.Precision.HIGHEST
        )
        residual = (
            select_group(live_weights, crop_position, 0)[None, :, None]
            * (ranked_crops - select_group(targets, crop_position, 1))
            / select_group(cell_counts, crop_position, 0)[None, :, None]
        )
        dbefore = jnp.where(before > 0, head_value[:, None, None, None] * residual[None], 0.0)
        return (normal, hidden, residual, dbefore)

    def backward_sums(number, running):
        first_sums, second_sums, vector_sums = running
        crop_position = number * slot_group
        normal, hidden, residual, dbefore = local_grads(crop_position)
        dnormal = dbefore * gain_value[:, None, None, None]
        first_sums = update_group(first_sums, jnp.sum(dnormal, (1, 3)), crop_position, 1)
        second_sums = update_group(second_sums, jnp.sum(dnormal * normal, (1, 3)), crop_position, 1)
        vector_terms = jnp.stack(
            [
                jnp.sum(dbefore * normal, (1, 2, 3)),
                jnp.sum(dbefore, (1, 2, 3)),
                jnp.sum(hidden * residual[None], (1, 2, 3)),
            ],
            1,
        )
        return (first_sums, second_sums, vector_sums + vector_terms)

    first_sums, second_sums, vector_grad = lax.fori_loop(
        0,
        groups,
        backward_sums,
        (empty_statistics, empty_statistics, jnp.zeros((out_channels, 3), jnp.float32)),
    )
    first_total, second_total = collect_batch_statistics((first_sums, second_sums))
    first_mean = first_total / cell_counts[None, :]
    second_mean = second_total / cell_counts[None, :]

    def weight_step(number, summed):
        crop_position = number * slot_group
        normal, hidden, residual, dbefore = local_grads(crop_position)
        dnormal = dbefore * gain_value[:, None, None, None]
        dfield = (
            select_group(live_weights, crop_position, 0)[None, None, :, None]
            * select_group(inverse_std, crop_position, 1)[:, None, :, None]
            * (
                dnormal
                - select_group(first_mean, crop_position, 1)[:, None, :, None]
                - normal * select_group(second_mean, crop_position, 1)[:, None, :, None]
            )
        )
        dfield = dfield.astype(jnp.bfloat16).reshape(out_channels, -1, columns)
        patches = plane_patches(crop_patches(crop_position), planes, crop_rows)
        moved = [column_shift(dfield, 1), dfield, column_shift(dfield, -1)]
        pieces = [
            lax.dot_general(
                part.reshape(out_channels, -1),
                patches,
                (((1,), (1,)), ((), ())),
                preferred_element_type=jnp.float32,
            )
            for part in moved
        ]
        return summed + jnp.stack(pieces, 0)

    tap_grad = lax.fori_loop(
        0, groups, weight_step, jnp.zeros((3, out_channels, 9 * channels), jnp.float32)
    )
    weight_grad = (
        tap_grad.reshape(3, out_channels, 9, channels)
        .transpose(1, 2, 0, 3)
        .reshape(out_channels, 27 * channels)
    )
    return (weight_grad, vector_grad)


def per_device(features, labels, crop_block, weight, gain, shift, head, run_mean, run_var):
    vectors = jnp.stack([gain, shift, head, run_mean, run_var], 1).astype(jnp.bfloat16)
    weight_b, vectors_b = sent_together((weight.astype(jnp.bfloat16), vectors), "dev", 0, 1)
    vector_f = vectors_b.astype(jnp.float32)
    gain_value = vector_f[:, 0]
    shift_value = vector_f[:, 1]
    head_value = vector_f[:, 2]
    mean_value = vector_f[:, 3]
    spread_value = vector_f[:, 4]
    out_channels = weight_b.shape[0]
    own_slab = features[0]
    channels, planes, height, columns = own_slab.shape
    weight_taps = (
        weight_b.reshape(out_channels, 9, 3, channels)
        .transpose(2, 0, 1, 3)
        .reshape(3, out_channels, 9 * channels)
    )
    bordered = extended(own_slab, (("dev", 1),), 1)
    padded = jnp.pad(bordered, ((0, 0), (0, 0), (1, 1), (0, 0)))
    inverse_std = lax.rsqrt(spread_value + epsilon)
    plane_scores = []
    for plane_index in range(planes):
        conv_out = conv_taps(padded[:, plane_index : plane_index + 3, None], weight_taps, 1, height)
        hidden = jax.nn.relu(
            gain_value[:, None] * (conv_out - mean_value[:, None]) * inverse_std[:, None]
            + shift_value[:, None]
        )
        plane_scores.append(
            jnp.dot(head_value, hidden, precision=lax.Precision.HIGHEST).reshape(height, columns)
        )
    scores = jnp.stack(plane_scores)[None]
    route_table = crop_block[0]
    slots = route_table.shape[0]
    own_index = lax.axis_index("dev")
    block_count = height // CY
    crop_cells = planes * CY * columns
    row_entries = lax.dynamic_slice_in_dim(route_table, own_index, 1, 0)[0]
    col_entries = lax.dynamic_slice_in_dim(route_table, own_index, 1, 1)[:, 0]
    send_live = row_entries >= 0
    chosen = jnp.maximum(row_entries, 0)
    slab_blocks = own_slab.reshape(channels, planes, block_count, CY, columns)
    send_crops = jnp.take(slab_blocks, chosen, axis=2)
    send_crops = jnp.where(
        send_live[None, None, :, None, None], send_crops, jnp.zeros((), jnp.bfloat16)
    )
    label_blocks = labels[0].reshape(1, planes, block_count, CY, columns)
    send_labels = jnp.take(label_blocks, chosen, axis=2)
    send_labels = jnp.where(
        send_live[None, None, :, None, None], send_labels, jnp.zeros((), jnp.bfloat16)
    )
    crop_data, crop_labels = (
        lax.all_to_all(send_crops, "dev", split_axis=2, concat_axis=2, tiled=True),
        lax.all_to_all(send_labels, "dev", split_axis=2, concat_axis=2, tiled=True),
    )
    live_flags = col_entries >= 0
    cell_counts = jnp.broadcast_to(jnp.sum(live_flags.astype(jnp.float32)), (slots,)) * crop_cells
    weight_terms, vector_terms = learn(
        crop_data,
        crop_labels[0],
        live_flags,
        cell_counts,
        weight_taps,
        gain_value,
        shift_value,
        head_value,
        local_total,
    )
    weight_part, vector_part = sent_together_2((weight_terms, vector_terms), "dev", 0, 1)
    weight_grad, vector_grad = in_one((weight_part, vector_part), "role")
    return (scores, weight_grad, vector_grad)


def solution(mesh):
    in_specs = (
        P("role", None, "dev", None, None),
        P("role", "dev", None, None),
        P("role", None, None),
        P("dev", None),
        P("dev"),
        P("dev"),
        P("dev"),
        P("dev"),
        P("dev"),
    )
    out_specs = (P("role", "dev", None, None), P("dev", None), P("dev", None))
    return jax.shard_map(
        per_device, mesh=mesh, in_specs=in_specs, out_specs=out_specs, check_vma=False
    )
```

profile of v0, /device:TPU:1, one launch (start us, length us, event | category | flops | bytes accessed | tf_op | source)
XLA Modules:
  0.0 757.6 jit_solution(12040742709633165185)
XLA Ops:
  12.4 15.1 %all-to-all-start.1 = ((bf16[1,2,64,4,128]{4,3,1,0,2:T(4,128)(2,1)}), bf16[1,2,64,4,128]{4,3,1,0,2:T(4,128)(2,1)S(1)}, u32[]{:S(2)}, u32[]{:S(2)}) async-start(bf16[1,2,64,4,128]{4,3,1,0,2:T(4,128)(2,1)} %fusion.109), calls=%async_computation.1 | async-start | bytes 262144 | tf_op jit(solution)/shard_map/all_to_all | solution.py:319
  34.3 96.6 %all-gather = bf16[64,1,869]{2,1,0:T(2,128)(2,1)S(1)} all-gather(bf16[1,1,869]{2,1,0:T(2,128)(2,1)S(1)} %bitcast.593), channel_id=1, replica_groups=mesh['role'=2,'dev'=64] {'dev'}, dimensions={0}, use_global_device_ids=true | all-gather | bytes 112970 | tf_op jit(solution)/shard_map/all_gather | solution.py:14
  148.1 5.4 all-to-all-start
  172.6 10.6 %add_bitcast_fusion.1 = f32[64,8,8,128]{3,2,1,0:T(8,128)S(1)} fusion(f32[64,64,127]{2,0,1:T(8,128)S(1)} %fusion.65, f32[64,64,127]{2,0,1:T(8,128)S(1)} %fusion.67, bf16[64,288,1]{0,1,2:T(8,128)(2,1)S(1)} %bitcast.565, bf16[36,8,64,128]{3,2,1,0:T(8,128)(2,1)S(1)} %bitcast.555), kind=kOutput, calls=%fused_computation.166 | convolution fusion | flops 303038464 | bytes 11014144 | tf_op jit(solution)/shard_map/dot_general | solution.py:98
  183.2 11.0 %add_bitcast_fusion = f32[64,8,8,128]{3,2,1,0:T(8,128)S(1)} fusion(f32[64,64,127]{2,0,1:T(8,128)S(1)} %fusion.61, f32[64,64,127]{2,0,1:T(8,128)S(1)} %fusion.63, bf16[64,288,1]{0,1,2:T(8,128)(2,1)S(1)} %bitcast.566, bf16[36,8,64,128]{3,2,1,0:T(8,128)(2,1)S(1)} %bitcast.553), kind=kOutput, calls=%fused_computation.165 | convolution fusion | flops 303038464 | bytes 11014144 | tf_op jit(solution)/shard_map/dot_general | solution.py:98
  197.9 9.1 %all-to-all-done = bf16[32,2,64,4,128]{4,0,3,1,2:T(8,128)(2,1)} async-done(((bf16[32,2,64,4,128]{4,0,3,1,2:T(8,128)(2,1)}), bf16[32,2,64,4,128]{4,0,3,1,2:T(8,128)(2,1)}, u32[]{:S(2)}, u32[]{:S(2)}) %all-to-all-start) | async-done | bytes 4194336 | tf_op jit(solution)/shard_map/all_to_all | solution.py:318
  207.0 5.7 copy.314
  212.7 5.2 gather_fusion.2
  217.9 6.3 copy.316
  228.5 125.5 %while.48 = (s32[]{:T(128)}, bf16[64,2,64,512]{3,2,1,0:T(8,128)(2,1)}, s32[]{:T(128)}, bf16[32,2,64,4,128]{4,3,2,1,0:T(4,128)(2,1)}, bf16[3,64,288]{2,1,0:T(8,12...) while((s32[]{:T(128)}, bf16[64,2,64,512]{3,2,1,0:T(8,128)(2,1)}, s32[]{:T(128)}, ...), condition=%wide.region_3.4_spmd, body=%wide.region_2.3_spmd.sunk | while | flops 907542528 | bytes 87638208 | solution.py:159
  240.8 8.8 %reshape.496 = bf16[288,8192]{1,0:T(8,128)(2,1)} reshape(bf16[9,32,2,8,4,128]{5,4,3,2,1,0:T(4,128)(2,1)} %fusion.198) | data formatting | bytes 9437184 | tf_op jit(solution)/shard_map/while/body/reshape | solution.py:91
  272.2 8.8 %reshape.496 = bf16[288,8192]{1,0:T(8,128)(2,1)} reshape(bf16[9,32,2,8,4,128]{5,4,3,2,1,0:T(4,128)(2,1)} %fusion.198) | data formatting | bytes 9437184 | tf_op jit(solution)/shard_map/while/body/reshape | solution.py:91
  303.5 8.8 %reshape.496 = bf16[288,8192]{1,0:T(8,128)(2,1)} reshape(bf16[9,32,2,8,4,128]{5,4,3,2,1,0:T(4,128)(2,1)} %fusion.198) | data formatting | bytes 9437184 | tf_op jit(solution)/shard_map/while/body/reshape | solution.py:91
  334.8 8.8 %reshape.496 = bf16[288,8192]{1,0:T(8,128)(2,1)} reshape(bf16[9,32,2,8,4,128]{5,4,3,2,1,0:T(4,128)(2,1)} %fusion.198) | data formatting | bytes 9437184 | tf_op jit(solution)/shard_map/while/body/reshape | solution.py:91
  354.0 5.4 convert_reduce_fusion
  363.0 9.2 %while.49 = (s32[]{:T(128)}, f32[64,64]{1,0:T(8,128)S(1)}, s32[]{:T(128)}, bf16[64,2,64,512]{3,2,1,0:T(8,128)(2,1)}, f32[64,64]{1,0:T(8,128)S(1)}, /*index=5*/f3...) while((s32[]{:T(128)}, f32[64,64]{1,0:T(8,128)S(1)}, s32[]{:T(128)}, ...), condition=%wide.region_10.11_spmd, body=%wide.region_8.10_spmd.sunk | while | flops 2620934 | bytes 1061131 | solution.py:180
  374.0 36.2 %while.50 = (s32[]{:T(128)}, f32[64,64]{1,0:T(8,128)S(1)}, f32[64,64]{1,0:T(8,128)S(1)}, f32[64,3]{0,1:T(4,128)S(1)}, s32[]{:T(128)}, /*index=5*/f32[64,1]{0,1:T...) while((s32[]{:T(128)}, f32[64,64]{1,0:T(8,128)S(1)}, ...), condition=%wide.region_19.20_spmd, body=%wide.region_13.19_spmd.sunk | while | flops 18898308 | bytes 6489027 | solution.py:219
  413.5 155.9 %while.51 = (s32[]{:T(128)}, f32[3,64,288]{2,1,0:T(8,128)S(1)}, s32[]{:T(128)}, f32[64]{0:T(128)S(1)}, f32[64,64]{1,0:T(8,128)S(1)}, /*index=5*/f32[64,1]{0,1:T(...) while((s32[]{:T(128)}, f32[3,64,288]{2,1,0:T(8,128)S(1)}, ...), condition=%wide.region_25.26_spmd, body=%wide.region_24.25_spmd.sunk | while | flops 922937856 | bytes 72345640 | solution.py:256
  426.0 8.8 %reshape.497 = bf16[288,8192]{1,0:T(8,128)(2,1)} reshape(bf16[9,32,2,8,4,128]{5,4,3,2,1,0:T(4,128)(2,1)} %fusion.220) | data formatting | bytes 9437184 | tf_op jit(solution)/shard_map/while/body/reshape | solution.py:91
  464.9 8.8 %reshape.497 = bf16[288,8192]{1,0:T(8,128)(2,1)} reshape(bf16[9,32,2,8,4,128]{5,4,3,2,1,0:T(4,128)(2,1)} %fusion.220) | data formatting | bytes 9437184 | tf_op jit(solution)/shard_map/while/body/reshape | solution.py:91
  503.7 8.8 %reshape.497 = bf16[288,8192]{1,0:T(8,128)(2,1)} reshape(bf16[9,32,2,8,4,128]{5,4,3,2,1,0:T(4,128)(2,1)} %fusion.220) | data formatting | bytes 9437184 | tf_op jit(solution)/shard_map/while/body/reshape | solution.py:91
  542.6 8.8 %reshape.497 = bf16[288,8192]{1,0:T(8,128)(2,1)} reshape(bf16[9,32,2,8,4,128]{5,4,3,2,1,0:T(4,128)(2,1)} %fusion.220) | data formatting | bytes 9437184 | tf_op jit(solution)/shard_map/while/body/reshape | solution.py:91
  570.5 167.8 %all-to-all-start.2 = ((f32[64,1,867]{2,1,0:T(1,128)}), f32[64,1,867]{2,1,0:T(1,128)S(1)}, u32[]{:S(2)}, u32[]{:S(2)}) async-start(f32[64,1,867]{2,1,0:T(1,128)} %copy.342), calls=%async_computation.2 | async-start | bytes 458752 | tf_op jit(solution)/shard_map/all_to_all | solution.py:45
  739.2 10.1 %all-to-all-done.2 = f32[64,1,867]{2,1,0:T(1,128)S(1)} async-done(((f32[64,1,867]{2,1,0:T(1,128)}), f32[64,1,867]{2,1,0:T(1,128)S(1)}, u32[]{:S(2)}, u32[]{:S(2)}) %all-to-all-start.2) | async-done | bytes 221984 | tf_op jit(solution)/shard_map/all_to_all | solution.py:45
  (425 shorter events, 330.6 us)
Async XLA Ops:
  0.6 10.2 %copy-start = (bf16[1,2,64,128]{3,2,1,0:T(8,128)(2,1)S(1)}, bf16[1,2,64,128]{3,2,1,0:T(8,128)(2,1)}, u32[]{:S(2)}) copy-start(bf16[1,2,64,128]{3,2,1,0:T(8,128)(2,1)} %param.18) | copy-start | bytes 98308
  0.6 30.3 %copy-start.13 = (f32[1,864]{1,0:T(1,128)S(1)}, f32[1,864]{1,0:T(1,128)}, u32[]{:S(2)}) copy-start(f32[1,864]{1,0:T(1,128)} %param.20) | copy-start | bytes 10372
  3.0 152.2 %collective-permute-start.1 = (bf16[32,1,64,128]{3,2,1,0:T(8,128)(2,1)}, bf16[32,1,64,128]{3,2,1,0:T(8,128)(2,1)S(1)}, u32[]{:S(2)}, u32[]{:S(2)}) collective-permute-start(bf16[32,1,64,128]{3,2,1,0:T(8,128)(2,1)} %get-tuple-element.751), channel_id=1, source_target_pairs={{1,0},{2,1},{3,2},{4,3},{5,4},{6,5},{7,6},{8,7},{9,8},{10,9},{11,1... | collective-permute-start | bytes 1572872 | tf_op jit(solution)/shard_map/ppermute | solution.py:31
  6.3 148.9 %collective-permute-start = (bf16[32,1,64,128]{3,2,1,0:T(8,128)(2,1)}, bf16[32,1,64,128]{3,2,1,0:T(8,128)(2,1)S(1)}, u32[]{:S(2)}, u32[]{:S(2)}) collective-permute-start(bf16[32,1,64,128]{3,2,1,0:T(8,128)(2,1)} %get-tuple-element.750), channel_id=1, source_target_pairs={{0,1},{1,2},{2,3},{3,4},{4,5},{5,6},{6,7},{7,8},{8,9},{9,10},{10,1... | collective-permute-start | bytes 1572872 | tf_op jit(solution)/shard_map/ppermute | solution.py:29
  12.4 135.6 %all-to-all-start.1 = ((bf16[1,2,64,4,128]{4,3,1,0,2:T(4,128)(2,1)}), bf16[1,2,64,4,128]{4,3,1,0,2:T(4,128)(2,1)S(1)}, u32[]{:S(2)}, u32[]{:S(2)}) async-start(bf16[1,2,64,4,128]{4,3,1,0,2:T(4,128)(2,1)} %fusion.109), calls=%async_computation.1 | async-start | bytes 262144 | tf_op jit(solution)/shard_map/all_to_all | solution.py:319
  141.5 6.5 copy-start.14
  148.0 48.5 %copy-start.11 = (bf16[64]{0:T(256)(128)(2,1)}, bf16[64]{0:T(256)(128)(2,1)S(1)}, u32[]{:S(2)}) copy-start(bf16[64]{0:T(256)(128)(2,1)S(1)} %slice_reduce_fusion.1) | copy-start | bytes 388
  148.0 7.2 copy-start.3
  148.1 58.9 %all-to-all-start = ((bf16[32,2,64,4,128]{4,0,3,1,2:T(8,128)(2,1)}), bf16[32,2,64,4,128]{4,0,3,1,2:T(8,128)(2,1)}, u32[]{:S(2)}, u32[]{:S(2)}) async-start(bf16[32,2,64,4,128]{4,0,3,1,2:T(8,128)(2,1)} %select_bitcast_fusion), calls=%async_computation | async-start | bytes 8388608 | tf_op jit(solution)/shard_map/all_to_all | solution.py:318
  361.1 12.8 %copy-start.5 = (f32[64,1]{0,1:T(1,128)S(1)}, f32[64,1]{0,1:T(1,128)}, u32[]{:S(2)}) copy-start(f32[64,1]{0,1:T(1,128)} %copy.332) | copy-start | bytes 772
  361.1 12.8 %copy-start.6 = (f32[64,1]{0,1:T(1,128)S(1)}, f32[64,1]{0,1:T(1,128)}, u32[]{:S(2)}) copy-start(f32[64,1]{0,1:T(1,128)} %copy.334) | copy-start | bytes 772
  361.1 12.8 %copy-start.8 = (f32[64]{0:T(128)S(1)}, f32[64]{0:T(128)}, u32[]{:S(2)}) copy-start(f32[64]{0:T(128)} %get-tuple-element.1183) | copy-start | bytes 772
  361.1 12.8 %copy-start.9 = (f32[64,1]{0,1:T(1,128)S(1)}, f32[64,1]{0,1:T(1,128)}, u32[]{:S(2)}) copy-start(f32[64,1]{0,1:T(1,128)} %copy.335) | copy-start | bytes 772
  413.5 324.9 %copy-start.12 = (bf16[64]{0:T(256)(128)(2,1)S(1)}, bf16[64]{0:T(256)(128)(2,1)}, u32[]{:S(2)}) copy-start(bf16[64]{0:T(256)(128)(2,1)} %copy-done.11) | copy-start | bytes 388
  443.5 5.3 slice-start
  443.9 4.9 slice-start.1
  482.3 5.3 slice-start
  521.2 5.3 slice-start
  560.0 5.3 slice-start
  569.4 169.0 %copy-start.4 = (f32[8,64,8,128]{3,2,1,0:T(8,128)S(1)}, f32[8,64,8,128]{3,2,1,0:T(8,128)}, u32[]{:S(2)}) copy-start(f32[8,64,8,128]{3,2,1,0:T(8,128)} %get-tuple-element.765) | copy-start | bytes 6291460
  569.4 184.1 %copy-start.7 = (f32[1,64,128]{2,0,1:T(1,128)S(1)}, f32[1,64,128]{2,0,1:T(1,128)}, u32[]{:S(2)}) copy-start(f32[1,64,128]{2,0,1:T(1,128)} %fusion.85) | copy-start | bytes 98308
  569.4 187.9 %copy-start.1 = (bf16[1,2,64,128]{3,2,1,0:T(8,128)(2,1)S(1)}, bf16[1,2,64,128]{3,2,1,0:T(8,128)(2,1)}, u32[]{:S(2)}) copy-start(bf16[1,2,64,128]{3,2,1,0:T(8,128)(2,1)} %param.18) | copy-start | bytes 98308
  570.5 178.8 %all-to-all-start.2 = ((f32[64,1,867]{2,1,0:T(1,128)}), f32[64,1,867]{2,1,0:T(1,128)S(1)}, u32[]{:S(2)}, u32[]{:S(2)}) async-start(f32[64,1,867]{2,1,0:T(1,128)} %copy.342), calls=%async_computation.2 | async-start | bytes 458752 | tf_op jit(solution)/shard_map/all_to_all | solution.py:45
  750.3 5.9 all-to-all-start.3
  (9 other events, 37.6 us)
where the time goes:
time: 769 us; the launch traced here: 758 us
  local copies, waits for them, and re-layouts  256 us (33%)
  starting transfers between devices  198 us (26%)
  matrix products  105 us (14%)
  blocking collectives  96.6 us (13%)
  other arithmetic  73 us (9%)
  waiting for transfers between devices  21.2 us (3%)
    all_to_all x1, starting transfers between devices, summed_on_arrival(): lax.all_to_all(in_blocks(array, dim, devices), axis, 0, 0, tiled=True)  168 us
    all_gather x1, blocking collectives, sent_together(): lax.all_gather(both, axis, axis=dim, tiled=True)  96.6 us
    while x104, local copies, waits for them, and re-layouts  86.2 us
    reshape x8, local copies, waits for them, and re-layouts, plane_patches(): return jnp.stack(shifted, 0).reshape(9 * padded.shape[0], -1)  70.5 us
    dot_general x18, matrix products, conv_taps(): jnp.dot(weight_taps[tap], patches, preferred_element_type=jnp.float32)  51.3 us
    dot_general x12, matrix products, weight_step(): lax.dot_general(part.reshape(out_channels, -1), patches, (((1,), (1,)), (...  30.4 us
    dot_general x8, matrix products, local_grads(): jnp.einsum('cpsk,c->psk', hidden, head_value, precision=lax.Precision.HIG...  18.9 us
  transfers between devices with their start and end apart: 6, of which 3 were waited for; matrix products, arithmetic and copies ran while one was open for 9% of the time, Pallas kernels for 0%

commit v1 on v0

v1 whole, which is shorter than its diff:
```python
import jax
import jax.numpy as jnp
from jax import lax
from jax.experimental import pallas as pl
from jax.experimental.pallas import tpu as pltpu
from jax.sharding import PartitionSpec as P


CY = 4
EPS = 1e-05
SENT = 48
F32 = jnp.float32
BF16 = jnp.bfloat16
PARAMS = pltpu.VMEM((512, 128), F32)
ANY = pl.BlockSpec(memory_space=pl.ANY)
VMEM = pl.BlockSpec(memory_space=pltpu.VMEM)
SMEM = pl.BlockSpec(memory_space=pltpu.SMEM)


def lane_iota(rows=64):
    return lax.broadcasted_iota(jnp.int32, (rows, 128), 1)


def roll_lanes(x, shift):
    shift %= 128
    return x if shift == 0 else pltpu.roll(x, shift, 1)


def load_params(w_ref, p_ref):
    wide = w_ref[...].astype(F32)
    p_ref[...] = wide.reshape(wide.shape[0] * 8, 128)


def chunk(p_ref, k):
    return p_ref[pl.ds(k, 64, stride=8), :]


def column(p_ref, k):
    return chunk(p_ref, 6)[:, 96 + k : 97 + k]


def fill_taps(p_ref, taps_ref):
    block = lane_iota() // 32
    chunks = [chunk(p_ref, k) for k in range(7)]
    for a in range(3):
        for c in range(3):
            out = jnp.zeros((64, 128), F32)
            for b in range(3):
                tap = 9 * a + 3 * b + c
                moved = roll_lanes(chunks[tap // 4], 32 * (b - tap % 4))
                out = jnp.where(block == b, moved, out)
            taps_ref[c, a] = out


def banded(taps_ref, c, a, yo):
    block = lane_iota() // 32
    v = roll_lanes(taps_ref[c, a], 32 * (yo - 1))
    if yo == 0:
        v = jnp.where(block == 3, 0.0, v)
    if yo == 3:
        v = jnp.where(block == 0, 0.0, v)
    return v


def pack_kernel(weight_ref, gain_ref, shift_ref, head_ref, mean_ref, var_ref, out_ref):
    lane = lax.broadcasted_iota(jnp.int32, (8, 128), 1)
    sub = lax.broadcasted_iota(jnp.int32, (8, 128), 0)
    out = jnp.zeros((8, 128), F32)
    for k in range(6):
        out = jnp.where(sub == k, weight_ref[:, 128 * k : 128 * k + 128], out)
    tail = jnp.concatenate([weight_ref[:, 768:864], jnp.zeros((1, 32), F32)], axis=1)
    out = jnp.where(sub == 6, tail, out)
    for k, ref in enumerate((gain_ref, shift_ref, head_ref, mean_ref, var_ref)):
        out = jnp.where((sub == 6) & (lane == 96 + k), ref[...].reshape(1, 1), out)
    out_ref[...] = jnp.broadcast_to(out.astype(BF16)[None], out_ref.shape)


def shifted(v):
    lane = lax.broadcasted_iota(jnp.int32, v.shape, 1)
    left = jnp.where(lane == 0, 0.0, pltpu.roll(v, 1, 1))
    right = jnp.where(lane == 127, 0.0, pltpu.roll(v, 127, 1))
    return left, v, right


def prep_kernel(slab_ref, x_ref, wide_ref):
    channels, _, height, _ = slab_ref.shape
    wide_ref[...] = slab_ref[:, 0].astype(F32).reshape(channels * height, 128)
    for y in range(height):
        v = wide_ref[pl.ds(y, channels, stride=height), :]
        rows = slice(32 * (y % CY), 32 * (y % CY) + 32)
        lanes = slice(128 * (y // CY), 128 * (y // CY) + 128)
        for c, w in enumerate(shifted(v)):
            x_ref[c, 0, rows, lanes] = w.astype(BF16)


def crop_conv_kernel(w_ref, x_ref, u_ref, stats_ref, p_ref, taps_ref, t_ref, s1_ref, m2_ref):
    load_params(w_ref, p_ref)
    fill_taps(p_ref, taps_ref)
    for zo in range(2):
        for yo in range(4):
            row = 64 * (4 * zo + yo)
            for c in range(3):
                for z in range(2):
                    col = 256 * c + 128 * z
                    v = banded(taps_ref, c, z - zo + 1, yo)
                    t_ref[row : row + 64, col : col + 128] = v.astype(BF16)
    s1_ref[...] = jnp.zeros((64, 128), F32)
    m2_ref[...] = jnp.zeros((64, 128), F32)
    lanes = lane_iota()

    def convolve(p):
        dst = pl.multiple_of(256 * p, 128)
        x = jnp.concatenate(
            [x_ref[c, z, :, pl.ds(dst, 256)] for c in range(3) for z in range(2)], axis=0
        )
        u = jnp.dot(t_ref[...], x, preferred_element_type=F32).astype(BF16)
        for half in range(2):
            for j in range(8):
                u_ref[pl.ds(pl.multiple_of(64 * (2 * p + half), 64), 64), 128 * j : 128 * j + 128] = u[
                    64 * j : 64 * j + 64, 128 * half : 128 * half + 128
                ]

    def statistics(p, u):
        for half in range(2):
            parts = [
                u[64 * half : 64 * half + 64, 128 * j : 128 * j + 128].astype(F32)
                for j in range(8)
            ]
            total = jnp.sum(sum(parts), axis=1, keepdims=True)
            mean = total * (1.0 / 1024)
            square = jnp.zeros((64, 128), F32)
            for part in parts:
                d = part - mean
                square = square + d * d
            here = lanes == 2 * p + half
            s1_ref[...] = jnp.where(here, total, s1_ref[...])
            m2_ref[...] = jnp.where(here, jnp.sum(square, axis=1, keepdims=True), m2_ref[...])

    convolve(0)

    def step(p, _):
        before = u_ref[pl.ds(pl.multiple_of(128 * p, 128), 128), :]
        convolve(p + 1)
        statistics(p, before)
        return 0

    pairs = u_ref.shape[0] // 128
    lax.fori_loop(0, pairs - 1, step, 0)
    statistics(pairs - 1, u_ref[128 * (pairs - 1) :, :])
    stats = jnp.concatenate([s1_ref[...], m2_ref[...]], axis=0).T[:16]

    def spread(s, _):
        stats_ref[s] = stats
        return 0

    lax.fori_loop(0, stats_ref.shape[0], spread, 0, unroll=8)


def score_kernel(
    w_ref, x_ref, below_ref, above_ref, cbt_ref, _, out_ref, hot_ref, p_ref, taps_ref, t_ref, f_ref
):
    learners, sources = cbt_ref.shape
    entries = hot_ref.shape[1]
    live = jnp.where(cbt_ref[...] >= 0, 1.0, 0.0)
    earlier = lax.broadcasted_iota(jnp.int32, (learners, learners), 1) < lax.broadcasted_iota(
        jnp.int32, (learners, learners), 0
    )
    place = jnp.dot(
        jnp.where(earlier, 1.0, 0.0).astype(BF16), live.astype(BF16), preferred_element_type=F32
    )
    place = jnp.where(live > 0, place, -1.0).astype(BF16)
    lane = lax.broadcasted_iota(jnp.int32, (sources, entries), 1)
    start = SENT * lax.broadcasted_iota(jnp.int32, (sources, entries), 0)
    expand = jnp.where((lane >= start) & (lane < start + SENT), 1.0, 0.0).astype(BF16)
    wanted = jnp.dot(place, expand, preferred_element_type=F32)
    slot = (lax.broadcasted_iota(jnp.int32, (8, entries), 1) % SENT).astype(F32)[0:1]
    hot_ref[...] = jnp.where(wanted == slot, 1.0, 0.0).astype(BF16)
    load_params(w_ref, p_ref)
    fill_taps(p_ref, taps_ref)
    block = lane_iota() // 32
    zero = jnp.zeros((64, 128), F32)
    for zo in range(2):
        for yo in range(4):
            row = slice(64 * (4 * zo + yo), 64 * (4 * zo + yo) + 64)
            for c in range(3):
                edges = []
                for zz in range(4):
                    a = zz - zo
                    inside = 0 <= a <= 2
                    v = banded(taps_ref, c, a, yo) if inside else zero
                    col = 128 * (4 * c + zz)
                    t_ref[row, col : col + 128] = v.astype(BF16)
                    odd = zz % 2
                    if inside and yo == 0:
                        v = roll_lanes(taps_ref[c, a], 64 * odd)
                        edges.append(jnp.where(block == 2 * odd, v, 0.0))
                    elif inside and yo == 3:
                        v = roll_lanes(taps_ref[c, a], 64 * odd - 32)
                        edges.append(jnp.where(block == 2 * odd + 1, v, 0.0))
                    else:
                        edges.append(zero)
                for k in range(2):
                    col = 1536 + 128 * (2 * c + k)
                    v = edges[2 * k] + edges[2 * k + 1]
                    t_ref[row, col : col + 128] = v.astype(BF16)
    gain, shift, head, mean, var = (column(p_ref, k) for k in range(5))
    alpha = gain * lax.rsqrt(var + EPS)
    beta = shift - mean * alpha
    alpha = jnp.broadcast_to(alpha, (64, 128))
    beta = jnp.broadcast_to(beta, (64, 128))
    head = jnp.broadcast_to(head, (64, 128))

    count = x_ref.shape[3] // 128
    empty = jnp.zeros((128, 128), BF16)
    for c in range(3):
        for zz in range(4):
            f_ref[c, zz, :, 0:128] = empty
            f_ref[c, zz, :, 128 * (count + 1) : 128 * (count + 2)] = empty
        for z in range(2):
            f_ref[c, 1 + z, :, 128 : 128 * (count + 1)] = x_ref[c, z]

    def halo(b, _):
        src = pl.multiple_of(128 * b, 128)
        dst = pl.multiple_of(128 * b + 128, 128)
        for zz, ref in ((0, below_ref), (3, above_ref)):
            v = ref[0, :, pl.ds(src, 128)].astype(F32)
            for c, w in enumerate(shifted(v)):
                f_ref[c, zz, :, pl.ds(dst, 128)] = w.astype(BF16)
        return 0

    lax.fori_loop(0, count, halo, 0)

    def step(p, _):
        at = pl.multiple_of(256 * p, 128)
        pairs = [(c, zz) for c in range(3) for zz in range(4)]
        rows = [f_ref[c, zz, :, pl.ds(at + 128, 256)] for c, zz in pairs]
        for c, zz in pairs:
            rows.append(f_ref[c, zz, 96:128, pl.ds(at, 256)])
            rows.append(f_ref[c, zz, 0:32, pl.ds(at + 256, 256)])
        out = jnp.dot(t_ref[...], jnp.concatenate(rows, axis=0), preferred_element_type=F32)
        for half in range(2):
            for j in range(8):
                v = out[64 * j : 64 * j + 64, 128 * half : 128 * half + 128]
                h = jnp.maximum(v * alpha + beta, 0.0) * head
                out_ref[j // 4, 2 * p + half, j % 4 : j % 4 + 1, :] = jnp.sum(
                    h, axis=0, keepdims=True
                )
        return 0

    lax.fori_loop(0, count // 2, step, 0)


def exact_dot(a, v):
    hi = v.astype(BF16)
    rest = v - hi.astype(F32)
    mid = rest.astype(BF16)
    low = (rest - mid.astype(F32)).astype(BF16)
    out = jnp.dot(a, low, preferred_element_type=F32)
    out = out + jnp.dot(a, mid, preferred_element_type=F32)
    return out + jnp.dot(a, hi, preferred_element_type=F32)


def learner_kernel(
    cb_ref, w_ref, r_ref, cbt_ref, u_ref, lab_ref,
    send_ref, g_ref, mr_ref, vec_ref, inv_ref, row_ref,
    p_ref, acc_ref, part_ref, coef_ref, scale_ref, al_ref, be_ref, hd_ref, r0_ref, ru_ref,
):
    load_params(w_ref, p_ref)
    lanes = lane_iota()
    learners, sources = cbt_ref.shape
    entries = r_ref.shape[0]
    lane = lax.broadcasted_iota(jnp.int32, (sources, entries), 1)
    source = lax.broadcasted_iota(jnp.int32, (sources, entries), 0)
    expand = jnp.where(lane // 16 == source, 1.0, 0.0).astype(BF16)
    wanted = jnp.dot(cbt_ref[...].astype(BF16), expand, preferred_element_type=F32)
    which = lax.broadcasted_iota(jnp.int32, (learners, entries), 1) % 16
    onehot = jnp.where(wanted == which.astype(F32), 1.0, 0.0).astype(BF16)
    number = jnp.sum(jnp.where(cbt_ref[...] >= 0, 1.0, 0.0), axis=1, keepdims=True)
    r = r_ref[...]
    means = r * (1.0 / 1024)
    centre = jnp.mean(means, axis=0, keepdims=True)
    d = means - centre
    rolled = pltpu.roll(d, 64, 1)
    low_half = lax.broadcasted_iota(jnp.int32, (entries, 128), 1) < 64
    v = jnp.where(low_half, d, means + rolled * rolled)
    p = exact_dot(onehot, v) / number
    first = jnp.where(lanes < 64, p, 0.0)
    mu = first + centre
    var = pltpu.roll(p, 64, 1) - first * first
    rstd = lax.rsqrt(jnp.maximum(var, 0.0) + EPS)
    both = jnp.where(lanes < 64, mu, pltpu.roll(rstd, 64, 1))
    both_t = jnp.concatenate([both, jnp.zeros((128 - learners, 128), F32)], axis=0).T
    mr_ref[...] = both_t
    inverse = jnp.broadcast_to(1.0 / (number * 1024.0), (learners, 128))
    inverse = jnp.concatenate([inverse, jnp.zeros((128 - learners, 128), F32)], axis=0).T
    inv_ref[...] = inverse[:8]
    row_ref[...] = jnp.full((8, 128), -1, jnp.int32)
    gain, shift, head = (jnp.broadcast_to(column(p_ref, k), (64, 128)) for k in range(3))
    alpha = gain * both_t[64:]
    al_ref[...] = alpha
    be_ref[...] = shift - alpha * both_t[:64]
    hd_ref[...] = head
    r0_ref[...] = jnp.zeros((64, 128), F32)
    ru_ref[...] = jnp.zeros((64, 128), F32)
    acc_ref[...] = jnp.zeros_like(acc_ref)
    part_ref[...] = jnp.zeros_like(part_ref)
    live = cb_ref[2 * learners]

    def reduce(k, e):
        here = lanes == k
        r0 = jnp.sum(part_ref[2 * e], axis=1, keepdims=True)
        rh = jnp.sum(part_ref[2 * e + 1], axis=1, keepdims=True)
        r0_ref[...] = jnp.where(here, r0, r0_ref[...])
        ru_ref[...] = jnp.where(here, rh, ru_ref[...])

    def fetch(k):
        t = cb_ref[jnp.minimum(k, live - 1)]
        index = jnp.full((64, 128), t, jnp.int32)
        inv = jnp.take_along_axis(inv_ref[...], index[:8], axis=1)
        al = jnp.take_along_axis(al_ref[...], index, axis=1)
        be = jnp.take_along_axis(be_ref[...], index, axis=1)
        return jnp.where(k < live, inv, 0.0), al, be, hd_ref[...] * al

    def keep(e, coefficients):
        scale_ref[e] = coefficients[0]
        for n in range(3):
            coef_ref[3 * e + n] = coefficients[1 + n]

    def learner(k, e):
        t = cb_ref[jnp.minimum(k, live - 1)]
        b = cb_ref[learners + t]
        at = pl.multiple_of(b * 128, 128)
        row = pl.multiple_of(b * 64, 64)
        row_ref[...] = jnp.where(lanes[:8] == t, b, row_ref[...])
        al, be, c1 = (coef_ref[3 * e + n] for n in range(3))
        inv = scale_ref[e, 0:1]
        hd = hd_ref[...]
        r0 = jnp.zeros((64, 128), F32)
        rh = jnp.zeros((64, 128), F32)
        for j in range(8):
            us = u_ref[pl.ds(row, 64), 128 * j : 128 * j + 128].astype(F32)
            h = jnp.maximum(us * al + be, 0.0)
            score = jnp.sum(h * hd, axis=0, keepdims=True)
            res = (score - lab_ref[b, j : j + 1, :]) * inv
            m = jnp.where(h > 0, res, 0.0)
            r0 = r0 + m
            rh = rh + h * res
            acc_ref[64 * j : 64 * j + 64, pl.ds(at, 128)] += c1 * m
        part_ref[2 * e] = r0
        part_ref[2 * e + 1] = rh

    def step(i, _):
        for e in range(2):
            reduce(2 * i - 2 + e, e)
        following = [fetch(2 * i + 2 + e) for e in range(2)]
        for e in range(2):
            learner(2 * i + e, e)
            keep(e, following[e])
        return 0

    for e in range(2):
        keep(e, fetch(e))
    steps = (live + 1) // 2
    lax.fori_loop(0, steps, step, 0)
    for e in range(2):
        reduce(2 * steps - 2 + e, e)
    r0 = r0_ref[...]
    r1 = (ru_ref[...] - shift * r0) / gain
    sends = send_ref.shape[1]
    out = jnp.concatenate([r0, r1], axis=0).T[:sends].astype(BF16)

    def spread(s, _):
        send_ref[s] = out
        return 0

    lax.fori_loop(0, send_ref.shape[0], spread, 0, unroll=8)
    dgain = jnp.sum(head * r1, axis=1, keepdims=True)
    dshift = jnp.sum(head * r0, axis=1, keepdims=True)
    dhead = jnp.sum(gain * r1 + shift * r0, axis=1, keepdims=True)
    vec_ref[...] = jnp.where(
        lanes == 96, dgain, jnp.where(lanes == 97, dshift, jnp.where(lanes == 98, dhead, 0.0))
    )
    g_ref[...] = acc_ref[...].astype(BF16)


def gradient_kernel(
    w_ref, r_ref, hot_ref, mr_ref, inv_ref, cb_ref, g_ref, u_ref, x_ref, vec_ref,
    out_ref, p_ref, full_ref, dt_ref, row_ref,
):
    load_params(w_ref, p_ref)
    learners = hot_ref.shape[0]
    total = jnp.dot(hot_ref[...], r_ref[...], preferred_element_type=F32)
    total = jnp.concatenate([total, jnp.zeros((128 - learners, 128), F32)], axis=0).T
    gain, head = (jnp.broadcast_to(column(p_ref, k), (64, 128)) for k in (0, 2))
    factor = gain * head * inv_ref[0:1, :]
    first = factor * total[:64]
    second = factor * total[64:]
    mu = mr_ref[:64]
    rstd = mr_ref[64:]
    slope = rstd * rstd * second
    offset = rstd * first - slope * mu
    row = cb_ref[0:1, :]

    def block(b, _):
        at = pl.multiple_of(b * 128, 128)
        row64 = pl.multiple_of(b * 64, 64)
        here = row == b
        e = jnp.broadcast_to(jnp.sum(jnp.where(here, offset, 0.0), axis=1, keepdims=True), (64, 128))
        f = jnp.broadcast_to(jnp.sum(jnp.where(here, slope, 0.0), axis=1, keepdims=True), (64, 128))
        for j in range(8):
            rows = slice(64 * j, 64 * j + 64)
            v = g_ref[rows, pl.ds(at, 128)].astype(F32) - e
            v = v - f * u_ref[pl.ds(row64, 64), 128 * j : 128 * j + 128].astype(F32)
            full_ref[rows, pl.ds(at, 128)] = v.astype(BF16)
        return 0

    lax.fori_loop(0, 16, block, 0)
    for c in range(3):
        dt_ref[:, 256 * c : 256 * c + 256] = lax.dot_general(
            full_ref[...],
            jnp.concatenate([x_ref[c, 0], x_ref[c, 1]], axis=0),
            (((1,), (1,)), ((), ())),
            preferred_element_type=F32,
        )
    blocks = lane_iota() // 32
    outs = [jnp.zeros((64, 128), F32) for _ in range(6)] + [vec_ref[...]]
    for c in range(3):
        for a in range(3):
            acc = jnp.zeros((64, 128), F32)
            for zo in range(2):
                z = zo + a - 1
                if not 0 <= z <= 1:
                    continue
                for yo in range(4):
                    j = 4 * zo + yo
                    col = 256 * c + 128 * z
                    v = roll_lanes(dt_ref[64 * j : 64 * j + 64, col : col + 128], -32 * (yo - 1))
                    if yo == 0:
                        v = jnp.where(blocks == 0, 0.0, v)
                    if yo == 3:
                        v = jnp.where(blocks == 2, 0.0, v)
                    acc = acc + v
            for b in range(3):
                tap = 9 * a + 3 * b + c
                k = tap // 4
                outs[k] = jnp.where(
                    blocks == tap % 4, roll_lanes(acc, 32 * (tap % 4 - b)), outs[k]
                )
    outs.append(jnp.zeros((64, 128), F32))
    for k in range(8):
        row_ref[pl.ds(k, 64, stride=8), :] = outs[k]
    packed = row_ref[...].astype(BF16)
    for role in range(out_ref.shape[0] // 512):
        out_ref[512 * role : 512 * role + 512, :] = packed


def finish_kernel(r_ref, weight_ref, vector_ref):
    total = jnp.sum(r_ref[...].astype(F32), axis=0)
    for k in range(6):
        weight_ref[:, 128 * k : 128 * k + 128] = total[k : k + 1]
    weight_ref[:, 768:864] = total[6:7, :96]
    vector_ref[...] = total[6:7, 96:99]


def per_device(features, labels, crop_block, weight, gain, shift, head, run_mean, run_var):
    devices = lax.axis_size("dev")
    roles = lax.axis_size("role")
    rows = pl.pallas_call(
        pack_kernel,
        out_shape=jax.ShapeDtypeStruct((devices, 8, 128), BF16),
        in_specs=[VMEM] * 6,
        out_specs=VMEM,
        name="pack",
    )(weight, gain, shift, head, run_mean, run_var)
    params = lax.all_to_all(rows, "dev", 0, 0, tiled=True)

    slab = features[0]
    channels, planes, height, columns = slab.shape
    count = height // CY
    cells = count * columns
    field = pl.pallas_call(
        prep_kernel,
        out_shape=jax.ShapeDtypeStruct((3, planes, CY * channels, cells), BF16),
        grid=(planes,),
        in_specs=[pl.BlockSpec((channels, 1, height, columns), lambda z: (0, z, 0, 0))],
        out_specs=pl.BlockSpec((3, 1, CY * channels, cells), lambda z: (0, z, 0, 0)),
        scratch_shapes=[pltpu.VMEM((channels * height, columns), F32)],
        cost_estimate=pl.CostEstimate(flops=10**7, bytes_accessed=4 << 20, transcendentals=0),
        name="prep",
    )(slab)

    table = crop_block[0]
    own_index = lax.axis_index("dev")
    mine = lax.dynamic_slice_in_dim(table, own_index, 1, 0)[0]
    live = mine >= 0
    places = jnp.arange(devices)
    before = jnp.sum(live[None, :] & (places[None, :] < places[:, None]), axis=1)
    at = live[None, :] & (before[None, :] == places[:, None])
    order = jnp.sum(jnp.where(at, places[None, :], 0), axis=1)
    lists = jnp.concatenate([order, mine, jnp.sum(live.astype(jnp.int32))[None]]).astype(jnp.int32)
    turned = table.T.astype(F32)
    targets = labels[0].reshape(planes, count, CY, columns).transpose(1, 0, 2, 3)
    targets = targets.reshape(count, planes * CY, columns).astype(F32)

    u, stats = pl.pallas_call(
        crop_conv_kernel,
        out_shape=(
            jax.ShapeDtypeStruct((64 * count, 1024), BF16),
            jax.ShapeDtypeStruct((devices, count, 128), F32),
        ),
        in_specs=[VMEM] * 2,
        out_specs=(VMEM, VMEM),
        scratch_shapes=[
            PARAMS,
            pltpu.VMEM((3, 3, 64, 128), F32),
            pltpu.VMEM((512, 768), BF16),
            pltpu.VMEM((64, 128), F32),
            pltpu.VMEM((64, 128), F32),
        ],
        cost_estimate=pl.CostEstimate(flops=2 * 512 * 768 * cells, bytes_accessed=8 << 20, transcendentals=0),
        name="crop_conv",
    )(params, field)

    gathered = lax.all_to_all(stats, "dev", 0, 0, tiled=True)
    gathered = gathered.reshape(devices * count, 128)
    plane = field[1]
    below = lax.ppermute(plane[-1:], "dev", [(i, i + 1) for i in range(devices - 1)])
    above = lax.ppermute(plane[:1], "dev", [(i + 1, i) for i in range(devices - 1)])

    send, g, mr, vec, inverse, mine_row = pl.pallas_call(
        learner_kernel,
        out_shape=(
            jax.ShapeDtypeStruct((devices, SENT, 128), BF16),
            jax.ShapeDtypeStruct((512, cells), BF16),
            jax.ShapeDtypeStruct((128, 128), F32),
            jax.ShapeDtypeStruct((64, 128), F32),
            jax.ShapeDtypeStruct((8, 128), F32),
            jax.ShapeDtypeStruct((8, 128), jnp.int32),
        ),
        in_specs=[SMEM] + [VMEM] * 5,
        out_specs=(VMEM,) * 6,
        scratch_shapes=[
            PARAMS,
            pltpu.VMEM((512, cells), F32),
            pltpu.VMEM((4, 64, 128), F32),
            pltpu.VMEM((6, 64, 128), F32),
            pltpu.VMEM((2, 8, 128), F32),
        ]
        + [pltpu.VMEM((64, 128), F32)] * 5,
        cost_estimate=pl.CostEstimate(flops=10**10, bytes_accessed=8 << 20, transcendentals=0),
        name="learner",
    )(lists, params, gathered, turned, u, targets)

    arrived = lax.all_to_all(send, "dev", 0, 0, tiled=True)

    scores, hot = pl.pallas_call(
        score_kernel,
        out_shape=(
            jax.ShapeDtypeStruct((planes, count, CY, columns), F32),
            jax.ShapeDtypeStruct((devices, devices * SENT), BF16),
        ),
        in_specs=[VMEM] * 5 + [ANY],
        out_specs=(VMEM, VMEM),
        scratch_shapes=[
            PARAMS,
            pltpu.VMEM((3, 3, 64, 128), F32),
            pltpu.VMEM((512, 2304), BF16),
            pltpu.VMEM((3, planes + 2, CY * channels, cells + 256), BF16),
        ],
        cost_estimate=pl.CostEstimate(flops=2 * 512 * 2304 * cells, bytes_accessed=8 << 20, transcendentals=0),
        name="score",
    )(params, field, below, above, turned, vec)

    final = pl.pallas_call(
        gradient_kernel,
        out_shape=jax.ShapeDtypeStruct((roles * devices * 8, 128), BF16),
        in_specs=[VMEM] * 10,
        out_specs=VMEM,
        scratch_shapes=[
            PARAMS,
            pltpu.VMEM((512, cells), BF16),
            pltpu.VMEM((512, 768), F32),
            pltpu.VMEM((512, 128), F32),
        ],
        cost_estimate=pl.CostEstimate(flops=2 * 512 * 768 * cells, bytes_accessed=8 << 20, transcendentals=0),
        name="gradient",
    )(
        params,
        arrived.reshape(devices * SENT, 128),
        hot, mr, inverse, mine_row, g, u, field, vec,
    )
    final = lax.all_to_all(
        final.reshape(roles * devices, 8, 128), ("role", "dev"), 0, 0, tiled=True
    )
    weight_grad, vector_grad = pl.pallas_call(
        finish_kernel,
        out_shape=(
            jax.ShapeDtypeStruct((1, 864), F32),
            jax.ShapeDtypeStruct((1, 3), F32),
        ),
        in_specs=[VMEM],
        out_specs=(VMEM, VMEM),
        name="finish",
    )(final)
    return (scores.reshape(1, planes, height, columns), weight_grad, vector_grad)


def solution(mesh):
    in_specs = (
        P("role", None, "dev", None, None),
        P("role", "dev", None, None),
        P("role", None, None),
        P("dev", None),
        P("dev"),
        P("dev"),
        P("dev"),
        P("dev"),
        P("dev"),
    )
    out_specs = (P("role", "dev", None, None), P("dev", None), P("dev", None))
    return jax.shard_map(
        per_device, mesh=mesh, in_specs=in_specs, out_specs=out_specs, check_vma=False
    )
```

time: 769 us -> 129 us (0.17); the launches traced: 758 us -> 128 us
  local copies, waits for them, and re-layouts: 256 us -> 5.42 us
  starting transfers between devices: 198 us -> 36.8 us
  matrix products: 105 us -> 0 us
  blocking collectives: 96.6 us -> 17.1 us
  other arithmetic: 73 us -> 2.76 us
  Pallas kernels: 0 us -> 47.1 us
    all_to_all x4 -> x3, starting transfers between devices: 192 us -> 31.3 us  [the longest x1 12.5 us: per_device(): params = lax.all_to_all(rows, 'dev', 0, 0, tiled=True)]
    dot_general x41 -> x0, matrix products: 105 us -> none  [the longest x18 51.3 us: conv_taps(): jnp.dot(weight_taps[tap], patches, preferred_element_type=jnp.float32)]
    all_gather x1 -> x0, blocking collectives: 96.6 us -> none  [sent_together(): lax.all_gather(both, axis, axis=dim, tiled=True)]
    while x116 -> x0, local copies, waits for them, and re-layouts: 95.9 us -> none
    reshape x16 -> x0, local copies, waits for them, and re-layouts: 75.3 us -> none  [the longest x8 70.5 us: plane_patches(): return jnp.stack(shifted, 0).reshape(9 * padded.shape[0], -1)]
    pallas_call x0 -> x7, Pallas kernels: none -> 47.1 us  [the longest x1 12.2 us: per_device(): pl.pallas_call(score_kernel, out_shape=(jax.ShapeDtypeStruct((planes, cou...]
    reduce_sum x15 -> x3, other arithmetic: 24.5 us -> 0.85 us  [the longest x1 0.63 us: per_device(): jnp.sum(live.astype(jnp.int32))[None]]
    all_to_all x0 -> x1, blocking collectives: none -> 17.1 us  [per_device(): lax.all_to_all(final.reshape(roles * devices, 8, 128), ('role', 'dev'), 0...]
  transfers between devices with their start and end apart: 6 -> 5, of which waited for: 3 -> 2; matrix products, arithmetic and copies ran while one was open for 9% -> 4% of each run, Pallas kernels for 0% -> 27%
where the time goes in v1:
time: 129 us; the launch traced here: 128 us
  Pallas kernels  47.1 us (37%)
  starting transfers between devices  36.8 us (29%)
  blocking collectives  17.1 us (13%)
  waiting for transfers between devices  14.8 us (11%)
  local copies, waits for them, and re-layouts  5.42 us (4%)
  between operations  4 us (3%)
  other arithmetic  2.76 us (2%)
    all_to_all x1, blocking collectives, per_device(): lax.all_to_all(final.reshape(roles * devices, 8, 128), ('role', 'dev'), 0...  17.1 us
    all_to_all x1, starting transfers between devices, per_device(): params = lax.all_to_all(rows, 'dev', 0, 0, tiled=True)  12.5 us
    pallas_call x1, Pallas kernels, per_device(): pl.pallas_call(score_kernel, out_shape=(jax.ShapeDtypeStruct((planes, cou...  12.2 us
    all_to_all x1, starting transfers between devices, per_device(): gathered = lax.all_to_all(stats, 'dev', 0, 0, tiled=True)  11.6 us
    pallas_call x1, Pallas kernels, per_device(): pl.pallas_call(learner_kernel, out_shape=(jax.ShapeDtypeStruct((devices,...  11.3 us
    all_to_all x1, waiting for transfers between devices, per_device(): gathered = lax.all_to_all(stats, 'dev', 0, 0, tiled=True)  11.3 us
    pallas_call x1, Pallas kernels, per_device(): pl.pallas_call(gradient_kernel, out_shape=jax.ShapeDtypeStruct((roles * d...  9 us
    pallas_call x1, Pallas kernels, per_device(): pl.pallas_call(crop_conv_kernel, out_shape=(jax.ShapeDtypeStruct((64 * co...  7.42 us
  transfers between devices with their start and end apart: 5, of which 2 were waited for; matrix products, arithmetic and copies ran while one was open for 4% of the time, Pallas kernels for 27%

profile of v1, /device:TPU:1, one launch (start us, length us, event | category | flops | bytes accessed | tf_op | source)
XLA Modules:
  0.0 127.9 jit_solution(7254236990126962961)
XLA Ops:
  3.9 1.4 %pack.1 = bf16[64,8,128]{2,1,0:T(8,128)(2,1)} custom-call(f32[1,864]{1,0:T(1,128)} %weight_ref.1, f32[1]{0:T(128)S(6)} %copy.16.gain_ref, f32[1]{0:T(128)S(6)} %copy.17.shift_ref, f32[1]{0:T(128)S(6)} %copy.18.head_ref, f32[1]{0:T(128)S(6)} %copy.19.mean_ref, f32[1]{0:T(128)S(6)} %copy.20.var_ref), custom_call_target="tpu_custom_call" | custom-call | tf_op jit(solution)/shard_map/pack/pallas_call | solution.py:468
  5.3 12.5 %all-to-all-start = ((bf16[64,8,128]{2,1,0:T(8,128)(2,1)}), bf16[64,8,128]{2,1,0:T(8,128)(2,1)S(1)}, u32[]{:S(2)}, u32[]{:S(2)}) async-start(bf16[64,8,128]{2,1,0:T(8,128)(2,1)} %pack.1), calls=%async_computation | async-start | bytes 262144 | tf_op jit(solution)/shard_map/all_to_all | solution.py:475
  17.8 4.0 %prep.1.x_ref = bf16[3,2,128,2048]{3,2,1,0:T(8,128)(2,1)} custom-call(bf16[32,2,64,128]{3,2,1,0:T(8,128)(2,1)} %bitcast.26), custom_call_target="tpu_custom_call" | custom-call | flops 10000000 | bytes 4194304 | tf_op jit(solution)/shard_map/prep/pallas_call | solution.py:481
  21.8 1.3 slice_bitcast_fusion
  23.1 3.5 %collective-permute-start = (bf16[1,128,2048]{2,1,0:T(8,128)(2,1)S(1)}, bf16[1,128,2048]{2,1,0:T(8,128)(2,1)S(1)}, u32[]{:S(2)}, u32[]{:S(2)}) collective-permute-start(bf16[1,128,2048]{2,1,0:T(8,128)(2,1)S(1)} %get-tuple-element.30), channel_id=1, source_target_pairs={{0,1},{1,2},{2,3},{3,4},{4,5},{5,6},{6,7},{7,8},{8,9},{9,10},{10,1... | collective-permute-start | bytes 1572872 | tf_op jit(solution)/shard_map/ppermute | solution.py:527
  26.6 1.9 %collective-permute-start.1 = (bf16[1,128,2048]{2,1,0:T(8,128)(2,1)S(1)}, bf16[1,128,2048]{2,1,0:T(8,128)(2,1)S(1)}, u32[]{:S(2)}, u32[]{:S(2)}) collective-permute-start(bf16[1,128,2048]{2,1,0:T(8,128)(2,1)S(1)} %get-tuple-element.29), channel_id=1, source_target_pairs={{1,0},{2,1},{3,2},{4,3},{5,4},{6,5},{7,6},{8,7},{9,8},{10,9},{11,1... | collective-permute-start | bytes 1572872 | tf_op jit(solution)/shard_map/ppermute | solution.py:528
  28.7 0.6 copy.15
  29.4 0.6 copy-done.1
  30.1 7.4 %crop_conv.1 = (bf16[1024,1024]{1,0:T(8,128)(2,1)}, f32[64,16,128]{2,1,0:T(8,128)}) custom-call(bf16[64,8,128]{2,1,0:T(8,128)(2,1)} %copy-done.1, bf16[3,2,128,2048]{3,2,1,0:T(8,128)(2,1)} %prep.1.x_ref), custom_call_target="tpu_custom_call" | custom-call | flops 1610612736 | bytes 8388608 | tf_op jit(solution)/shard_map/crop_conv/pallas_call | solution.py:505
  37.5 11.6 %all-to-all-start.1 = ((f32[64,16,128]{2,1,0:T(8,128)}), f32[64,16,128]{2,1,0:T(8,128)S(1)}, u32[]{:S(2)}, u32[]{:S(2)}) async-start(f32[64,16,128]{2,1,0:T(8,128)} %get-tuple-element.15), calls=%async_computation.1 | async-start | bytes 1048576 | tf_op jit(solution)/shard_map/all_to_all | solution.py:524
  49.1 0.6 convert_reduce_fusion.1
  49.9 1.3 %pad_add_fusion.cb_ref = s32[129]{0:T(256)} fusion(s32[1]{0:T(128)} %bitcast.6, s32[64]{0:T(128)S(1)} %get-tuple-element.28, s32[64]{0:T(128)S(1)} %select_reduce_fusion), kind=kLoop, calls=%fused_computation.9 | loop fusion | flops 258 | bytes 1032 | tf_op jit(solution)/shard_map/concatenate | solution.py:500
  51.2 0.6 convert_bitcast_fusion.cbt_ref
  51.8 11.3 %all-to-all-done.1 = f32[64,16,128]{2,1,0:T(8,128)S(1)} async-done(((f32[64,16,128]{2,1,0:T(8,128)}), f32[64,16,128]{2,1,0:T(8,128)S(1)}, u32[]{:S(2)}, u32[]{:S(2)}) %all-to-all-start.1) | async-done | bytes 524320 | tf_op jit(solution)/shard_map/all_to_all | solution.py:524
  63.1 0.9 copy-done.2
  63.9 11.3 %learner.1 = (bf16[64,48,128]{2,1,0:T(8,128)(2,1)}, bf16[512,2048]{1,0:T(8,128)(2,1)}, f32[128,128]{1,0:T(8,128)}, f32[64,128]{1,0:T(8,128)}, f32[8,128]{1,0:T(8,128)}, /*index=5*/s32[8,128]{1,0:T(8,128)}) custom-call(s32[129]{0:T(256)} %pad_add_fusion.cb_ref, bf16[64,8,128]{2,1,0:T(8,128)(2,1)} %copy-done.1, f32[1024,128]{1,0:T(8,128)} %bitcast.27, ...), custom_call_target="tpu_custom_call" | custom-call | flops 10000000000 | bytes 8388608 | tf_op jit(solution)/shard_map/learner/pallas_call | solution.py:530
  75.3 7.3 %all-to-all-start.2 = ((bf16[64,48,128]{2,1,0:T(8,128)(2,1)}), bf16[64,48,128]{2,1,0:T(8,128)(2,1)S(1)}, u32[]{:S(2)}, u32[]{:S(2)}) async-start(bf16[64,48,128]{2,1,0:T(8,128)(2,1)} %get-tuple-element.19), calls=%async_computation.2 | async-start | bytes 1572864 | tf_op jit(solution)/shard_map/all_to_all | solution.py:554
  82.6 0.8 copy-done.5
  83.6 12.2 %score.1 = (f32[2,16,4,128]{3,2,1,0:T(4,128)}, bf16[64,3072]{1,0:T(8,128)(2,1)}) custom-call(bf16[64,8,128]{2,1,0:T(8,128)(2,1)} %copy-done.1, bf16[3,2,128,2048]{3,2,1,0:T(8,128)(2,1)} %prep.1.x_ref, bf16[1,128,2048]{2,1,0:T(8,128)(2,1)} %copy-done.5, bf16[1,128,2048]{2,1,0:T(8,128)(2,1)} %copy-done.6, f32[64,64]{1,0:T(8,128)} %convert_bitcast_fusion.cbt_ref, ...), custom_call_target="tpu_custom_call" | custom-call | flops 4831838208 | bytes 8388608 | tf_op jit(solution)/shard_map/score/pallas_call | solution.py:556
  95.8 3.5 %all-to-all-done.2 = bf16[64,48,128]{2,1,0:T(8,128)(2,1)S(1)} async-done(((bf16[64,48,128]{2,1,0:T(8,128)(2,1)}), bf16[64,48,128]{2,1,0:T(8,128)(2,1)S(1)}, u32[]{:S(2)}, u32[]{:S(2)}) %all-to-all-start.2) | async-done | bytes 786464 | tf_op jit(solution)/shard_map/all_to_all | solution.py:554
  99.3 0.9 copy-done
  100.2 9.0 %gradient.1 = bf16[1024,128]{1,0:T(8,128)(2,1)} custom-call(bf16[64,8,128]{2,1,0:T(8,128)(2,1)} %copy-done.1, bf16[3072,128]{1,0:T(8,128)(2,1)} %bitcast.24, bf16[64,3072]{1,0:T(8,128)(2,1)} %get-tuple-element.20.hot_ref, f32[128,128]{1,0:T(8,128)} %get-tuple-element.21.mr_ref, f32[8,128]{1,0:T(8,128)} %get-tuple-element.22.inv_ref, ...), custom_call_target="tpu_custom_call" | custom-call | flops 1610612736 | bytes 8388608 | tf_op jit(solution)/shard_map/gradient/pallas_call | solution.py:574
  109.2 17.1 %all_to_all.20.r_ref = bf16[128,8,128]{2,1,0:T(8,128)(2,1)} all-to-all(bf16[128,8,128]{2,1,0:T(8,128)(2,1)} %bitcast.25), channel_id=1, replica_groups=mesh['role'=2,'dev'=64] {'role','dev'}, dimensions={0} | all-to-all | bytes 524288 | tf_op jit(solution)/shard_map/all_to_all | solution.py:592
  126.3 1.7 %finish.1 = (f32[1,864]{1,0:T(1,128)}, f32[1,3]{1,0:T(1,128)}) custom-call(bf16[128,8,128]{2,1,0:T(8,128)(2,1)} %all_to_all.20.r_ref), custom_call_target="tpu_custom_call" | custom-call | tf_op jit(solution)/shard_map/finish/pallas_call | solution.py:595
  (17 shorter events, 0.5 us)
Async XLA Ops:
  5.3 24.1 %all-to-all-start = ((bf16[64,8,128]{2,1,0:T(8,128)(2,1)}), bf16[64,8,128]{2,1,0:T(8,128)(2,1)S(1)}, u32[]{:S(2)}, u32[]{:S(2)}) async-start(bf16[64,8,128]{2,1,0:T(8,128)(2,1)} %pack.1), calls=%async_computation | async-start | bytes 262144 | tf_op jit(solution)/shard_map/all_to_all | solution.py:475
  17.7 10.8 %copy-start.3 = (s32[1,64,64]{2,1,0:T(8,128)S(1)}, s32[1,64,64]{2,1,0:T(8,128)}, u32[]{:S(2)}) copy-start(s32[1,64,64]{2,1,0:T(8,128)} %param.11) | copy-start | bytes 49156
  17.8 10.9 %copy-start.4 = (bf16[1,2,64,128]{3,2,1,0:T(8,128)(2,1)S(1)}, bf16[1,2,64,128]{3,2,1,0:T(8,128)(2,1)}, u32[]{:S(2)}) copy-start(bf16[1,2,64,128]{3,2,1,0:T(8,128)(2,1)} %param.10) | copy-start | bytes 98308
  23.1 59.5 %collective-permute-start = (bf16[1,128,2048]{2,1,0:T(8,128)(2,1)S(1)}, bf16[1,128,2048]{2,1,0:T(8,128)(2,1)S(1)}, u32[]{:S(2)}, u32[]{:S(2)}) collective-permute-start(bf16[1,128,2048]{2,1,0:T(8,128)(2,1)S(1)} %get-tuple-element.30), channel_id=1, source_target_pairs={{0,1},{1,2},{2,3},{3,4},{4,5},{5,6},{6,7},{7,8},{8,9},{9,10},{10,1... | collective-permute-start | bytes 1572872 | tf_op jit(solution)/shard_map/ppermute | solution.py:527
  26.6 55.9 %collective-permute-start.1 = (bf16[1,128,2048]{2,1,0:T(8,128)(2,1)S(1)}, bf16[1,128,2048]{2,1,0:T(8,128)(2,1)S(1)}, u32[]{:S(2)}, u32[]{:S(2)}) collective-permute-start(bf16[1,128,2048]{2,1,0:T(8,128)(2,1)S(1)} %get-tuple-element.29), channel_id=1, source_target_pairs={{1,0},{2,1},{3,2},{4,3},{5,4},{6,5},{7,6},{8,7},{9,8},{10,9},{11,1... | collective-permute-start | bytes 1572872 | tf_op jit(solution)/shard_map/ppermute | solution.py:528
  29.4 0.7 copy-start.1
  37.5 25.6 %all-to-all-start.1 = ((f32[64,16,128]{2,1,0:T(8,128)}), f32[64,16,128]{2,1,0:T(8,128)S(1)}, u32[]{:S(2)}, u32[]{:S(2)}) async-start(f32[64,16,128]{2,1,0:T(8,128)} %get-tuple-element.15), calls=%async_computation.1 | async-start | bytes 1048576 | tf_op jit(solution)/shard_map/all_to_all | solution.py:524
  63.1 0.9 copy-start.2
  75.3 24.0 %all-to-all-start.2 = ((bf16[64,48,128]{2,1,0:T(8,128)(2,1)}), bf16[64,48,128]{2,1,0:T(8,128)(2,1)S(1)}, u32[]{:S(2)}, u32[]{:S(2)}) async-start(bf16[64,48,128]{2,1,0:T(8,128)(2,1)} %get-tuple-element.19), calls=%async_computation.2 | async-start | bytes 1572864 | tf_op jit(solution)/shard_map/all_to_all | solution.py:554
  82.5 0.9 copy-start.5
  82.6 1.0 copy-start.6
  99.3 0.9 copy-start

commit v2 on v1

--- a/solution.py
+++ b/solution.py
@@ -14,7 +14,18 @@
 PARAMS = pltpu.VMEM((512, 128), F32)
 ANY = pl.BlockSpec(memory_space=pl.ANY)
 VMEM = pl.BlockSpec(memory_space=pltpu.VMEM)
+SMALL = pltpu.CompilerParams(vmem_limit_bytes=20 << 20)
+HBM = pl.BlockSpec(memory_space=pltpu.HBM)
+DMA = pltpu.SemaphoreType.DMA
 SMEM = pl.BlockSpec(memory_space=pltpu.SMEM)
+
+
+def near(x):
+    return pltpu.with_memory_space_constraint(x, pltpu.VMEM)
+
+
+def far(x):
+    return pltpu.with_memory_space_constraint(x, pltpu.HBM)
 
 
 def lane_iota(rows=64):
@@ -62,16 +73,11 @@
     return v
 
 
-def pack_kernel(weight_ref, gain_ref, shift_ref, head_ref, mean_ref, var_ref, out_ref):
-    lane = lax.broadcasted_iota(jnp.int32, (8, 128), 1)
+def pack_kernel(row_ref, out_ref):
     sub = lax.broadcasted_iota(jnp.int32, (8, 128), 0)
     out = jnp.zeros((8, 128), F32)
-    for k in range(6):
-        out = jnp.where(sub == k, weight_ref[:, 128 * k : 128 * k + 128], out)
-    tail = jnp.concatenate([weight_ref[:, 768:864], jnp.zeros((1, 32), F32)], axis=1)
-    out = jnp.where(sub == 6, tail, out)
-    for k, ref in enumerate((gain_ref, shift_ref, head_ref, mean_ref, var_ref)):
-        out = jnp.where((sub == 6) & (lane == 96 + k), ref[...].reshape(1, 1), out)
+    for k in range(7):
+        out = jnp.where(sub == k, row_ref[:, 128 * k : 128 * k + 128], out)
     out_ref[...] = jnp.broadcast_to(out.astype(BF16)[None], out_ref.shape)
 
 
@@ -93,7 +99,9 @@
             x_ref[c, 0, rows, lanes] = w.astype(BF16)
 
 
-def crop_conv_kernel(w_ref, x_ref, u_ref, stats_ref, p_ref, taps_ref, t_ref, s1_ref, m2_ref):
+def crop_conv_kernel(
+    w_ref, x_ref, out_ref, stats_ref, p_ref, taps_ref, t_ref, s1_ref, m2_ref, u_ref, sem
+):
     load_params(w_ref, p_ref)
     fill_taps(p_ref, taps_ref)
     for zo in range(2):
@@ -119,6 +127,12 @@
                 u_ref[pl.ds(pl.multiple_of(64 * (2 * p + half), 64), 64), 128 * j : 128 * j + 128] = u[
                     64 * j : 64 * j + 64, 128 * half : 128 * half + 128
                 ]
+
+        leave(p).start()
+
+    def leave(p):
+        rows = pl.ds(pl.multiple_of(128 * p, 128), 128)
+        return pltpu.make_async_copy(u_ref.at[rows], out_ref.at[rows], sem.at[p])
 
     def statistics(p, u):
         for half in range(2):
@@ -154,11 +168,20 @@
         return 0
 
     lax.fori_loop(0, stats_ref.shape[0], spread, 0, unroll=8)
+    for p in range(8):
+        leave(p).wait()
 
 
 def score_kernel(
-    w_ref, x_ref, below_ref, above_ref, cbt_ref, _, out_ref, hot_ref, p_ref, taps_ref, t_ref, f_ref
+    w_ref, x_ref, below_ref, above_ref, cbt_ref, _, out_ref, hot_ref, p_ref, taps_ref, t_ref, f_ref, sem
 ):
+    count = x_ref.shape[3] // 128
+    arrive = []
+    for c in range(3):
+        for z in range(2):
+            inside = f_ref.at[c, 1 + z, :, pl.ds(128, 128 * count)]
+            arrive.append(pltpu.make_async_copy(x_ref.at[c, z], inside, sem.at[2 * c + z]))
+            arrive[-1].start()
     learners, sources = cbt_ref.shape
     entries = hot_ref.shape[1]
     live = jnp.where(cbt_ref[...] >= 0, 1.0, 0.0)
@@ -210,14 +233,11 @@
     beta = jnp.broadcast_to(beta, (64, 128))
     head = jnp.broadcast_to(head, (64, 128))
 
-    count = x_ref.shape[3] // 128
     empty = jnp.zeros((128, 128), BF16)
     for c in range(3):
         for zz in range(4):
             f_ref[c, zz, :, 0:128] = empty
             f_ref[c, zz, :, 128 * (count + 1) : 128 * (count + 2)] = empty
-        for z in range(2):
-            f_ref[c, 1 + z, :, 128 : 128 * (count + 1)] = x_ref[c, z]
 
     def halo(b, _):
         src = pl.multiple_of(128 * b, 128)
@@ -229,6 +249,8 @@
         return 0
 
     lax.fori_loop(0, count, halo, 0)
+    for copy in arrive:
+        copy.wait()
 
     def step(p, _):
         at = pl.multiple_of(256 * p, 128)
@@ -261,10 +283,13 @@
 
 
 def learner_kernel(
-    cb_ref, w_ref, r_ref, cbt_ref, u_ref, lab_ref,
-    send_ref, g_ref, mr_ref, vec_ref, inv_ref, row_ref,
+    cb_ref, w_ref, r_ref, cbt_ref, u_in_ref, lab_ref,
+    send_out_ref, g_out_ref, mr_ref, vec_ref, inv_ref, row_ref,
     p_ref, acc_ref, part_ref, coef_ref, scale_ref, al_ref, be_ref, hd_ref, r0_ref, ru_ref,
+    u_ref, send_ref, g_ref, sem,
 ):
+    arrive = pltpu.make_async_copy(u_in_ref, u_ref, sem.at[0])
+    arrive.start()
     load_params(w_ref, p_ref)
     lanes = lane_iota()
     learners, sources = cbt_ref.shape
@@ -305,6 +330,7 @@
     acc_ref[...] = jnp.zeros_like(acc_ref)
     part_ref[...] = jnp.zeros_like(part_ref)
     live = cb_ref[2 * learners]
+    arrive.wait()
 
     def reduce(k, e):
         here = lanes == k
@@ -374,19 +400,36 @@
         return 0
 
     lax.fori_loop(0, send_ref.shape[0], spread, 0, unroll=8)
+    send = pltpu.make_async_copy(send_ref, send_out_ref, sem.at[1])
+    send.start()
+    leaves = []
+    for j in range(8):
+        rows = slice(64 * j, 64 * j + 64)
+        g_ref[rows, :] = acc_ref[rows, :].astype(BF16)
+        leaves.append(pltpu.make_async_copy(g_ref.at[rows], g_out_ref.at[rows], sem.at[2 + j]))
+        leaves[j].start()
     dgain = jnp.sum(head * r1, axis=1, keepdims=True)
     dshift = jnp.sum(head * r0, axis=1, keepdims=True)
     dhead = jnp.sum(gain * r1 + shift * r0, axis=1, keepdims=True)
     vec_ref[...] = jnp.where(
         lanes == 96, dgain, jnp.where(lanes == 97, dshift, jnp.where(lanes == 98, dhead, 0.0))
     )
-    g_ref[...] = acc_ref[...].astype(BF16)
+    send.wait()
+    for leave in leaves:
+        leave.wait()
 
 
 def gradient_kernel(
-    w_ref, r_ref, hot_ref, mr_ref, inv_ref, cb_ref, g_ref, u_ref, x_ref, vec_ref,
-    out_ref, p_ref, full_ref, dt_ref, row_ref,
+    w_ref, r_ref, hot_ref, mr_ref, inv_ref, cb_ref, vec_ref, g_in_ref, u_in_ref, x_in_ref,
+    out_ref, p_ref, full_ref, dt_ref, row_ref, g_ref, u_ref, x_ref, sem,
 ):
+    arrive = [
+        pltpu.make_async_copy(g_in_ref, g_ref, sem.at[0]),
+        pltpu.make_async_copy(u_in_ref, u_ref, sem.at[1]),
+    ]
+    arrive += [pltpu.make_async_copy(x_in_ref.at[c], x_ref.at[c], sem.at[2 + c]) for c in range(3)]
+    for copy in arrive:
+        copy.start()
     load_params(w_ref, p_ref)
     learners = hot_ref.shape[0]
     total = jnp.dot(hot_ref[...], r_ref[...], preferred_element_type=F32)
@@ -414,8 +457,11 @@
             full_ref[rows, pl.ds(at, 128)] = v.astype(BF16)
         return 0
 
+    arrive[0].wait()
+    arrive[1].wait()
     lax.fori_loop(0, 16, block, 0)
     for c in range(3):
+        arrive[2 + c].wait()
         dt_ref[:, 256 * c : 256 * c + 256] = lax.dot_general(
             full_ref[...],
             jnp.concatenate([x_ref[c, 0], x_ref[c, 1]], axis=0),
@@ -465,14 +511,18 @@
 def per_device(features, labels, crop_block, weight, gain, shift, head, run_mean, run_var):
     devices = lax.axis_size("dev")
     roles = lax.axis_size("role")
+    row = jnp.pad(weight, ((0, 0), (0, 896 - 864)))
+    vectors = jnp.concatenate([gain, shift, head, run_mean, run_var])
+    row = row + jnp.pad(vectors[None], ((0, 0), (864, 27)))
     rows = pl.pallas_call(
         pack_kernel,
         out_shape=jax.ShapeDtypeStruct((devices, 8, 128), BF16),
-        in_specs=[VMEM] * 6,
+        in_specs=[VMEM],
         out_specs=VMEM,
+        compiler_params=SMALL,
         name="pack",
-    )(weight, gain, shift, head, run_mean, run_var)
-    params = lax.all_to_all(rows, "dev", 0, 0, tiled=True)
+    )(row)
+    params = near(lax.all_to_all(rows, "dev", 0, 0, tiled=True))
 
     slab = features[0]
     channels, planes, height, columns = slab.shape
@@ -480,16 +530,42 @@
     cells = count * columns
     field = pl.pallas_call(
         prep_kernel,
-        out_shape=jax.ShapeDtypeStruct((3, planes, CY * channels, cells), BF16),
+        out_shape=pltpu.VMEM((3, planes, CY * channels, cells), BF16),
         grid=(planes,),
         in_specs=[pl.BlockSpec((channels, 1, height, columns), lambda z: (0, z, 0, 0))],
         out_specs=pl.BlockSpec((3, 1, CY * channels, cells), lambda z: (0, z, 0, 0)),
         scratch_shapes=[pltpu.VMEM((channels * height, columns), F32)],
         cost_estimate=pl.CostEstimate(flops=10**7, bytes_accessed=4 << 20, transcendentals=0),
+        compiler_params=SMALL,
         name="prep",
     )(slab)
 
-    table = crop_block[0]
+    targets = labels[0].reshape(planes, count, CY, columns).transpose(1, 0, 2, 3)
+    targets = targets.reshape(count, planes * CY, columns).astype(F32)
+
+    u, stats = pl.pallas_call(
+        crop_conv_kernel,
+        out_shape=(
+            pltpu.HBM((64 * count, 1024), BF16),
+            pltpu.HBM((devices, count, 128), F32),
+        ),
+        in_specs=[VMEM] * 2,
+        out_specs=(HBM, VMEM),
+        scratch_shapes=[
+            PARAMS,
+            pltpu.VMEM((3, 3, 64, 128), F32),
+            pltpu.VMEM((512, 768), BF16),
+            pltpu.VMEM((64, 128), F32),
+            pltpu.VMEM((64, 128), F32),
+            pltpu.VMEM((64 * count, 1024), BF16),
+            DMA((8,)),
+        ],
+        cost_estimate=pl.CostEstimate(flops=2 * 512 * 768 * cells, bytes_accessed=8 << 20, transcendentals=0),
+        compiler_params=SMALL,
+        name="crop_conv",
+    )(params, near(field))
+
+    table, _ = lax.optimization_barrier((crop_block[0], stats))
     own_index = lax.axis_index("dev")
     mine = lax.dynamic_slice_in_dim(table, own_index, 1, 0)[0]
     live = mine >= 0
@@ -499,28 +575,6 @@
     order = jnp.sum(jnp.where(at, places[None, :], 0), axis=1)
     lists = jnp.concatenate([order, mine, jnp.sum(live.astype(jnp.int32))[None]]).astype(jnp.int32)
     turned = table.T.astype(F32)
-    targets = labels[0].reshape(planes, count, CY, columns).transpose(1, 0, 2, 3)
-    targets = targets.reshape(count, planes * CY, columns).astype(F32)
-
-    u, stats = pl.pallas_call(
-        crop_conv_kernel,
-        out_shape=(
-            jax.ShapeDtypeStruct((64 * count, 1024), BF16),
-            jax.ShapeDtypeStruct((devices, count, 128), F32),
-        ),
-        in_specs=[VMEM] * 2,
-        out_specs=(VMEM, VMEM),
-        scratch_shapes=[
-            PARAMS,
-            pltpu.VMEM((3, 3, 64, 128), F32),
-            pltpu.VMEM((512, 768), BF16),
-            pltpu.VMEM((64, 128), F32),
-            pltpu.VMEM((64, 128), F32),
-        ],
-        cost_estimate=pl.CostEstimate(flops=2 * 512 * 768 * cells, bytes_accessed=8 << 20, transcendentals=0),
-        name="crop_conv",
-    )(params, field)
-
     gathered = lax.all_to_all(stats, "dev", 0, 0, tiled=True)
     gathered = gathered.reshape(devices * count, 128)
     plane = field[1]
@@ -530,15 +584,15 @@
     send, g, mr, vec, inverse, mine_row = pl.pallas_call(
         learner_kernel,
         out_shape=(
-            jax.ShapeDtypeStruct((devices, SENT, 128), BF16),
-            jax.ShapeDtypeStruct((512, cells), BF16),
+            pltpu.HBM((devices, SENT, 128), BF16),
+            pltpu.HBM((512, cells), BF16),
             jax.ShapeDtypeStruct((128, 128), F32),
             jax.ShapeDtypeStruct((64, 128), F32),
             jax.ShapeDtypeStruct((8, 128), F32),
             jax.ShapeDtypeStruct((8, 128), jnp.int32),
         ),
-        in_specs=[SMEM] + [VMEM] * 5,
-        out_specs=(VMEM,) * 6,
+        in_specs=[SMEM] + [VMEM] * 3 + [HBM, VMEM],
+        out_specs=(HBM, HBM) + (VMEM,) * 4,
         scratch_shapes=[
             PARAMS,
             pltpu.VMEM((512, cells), F32),
@@ -546,10 +600,17 @@
             pltpu.VMEM((6, 64, 128), F32),
             pltpu.VMEM((2, 8, 128), F32),
         ]
-        + [pltpu.VMEM((64, 128), F32)] * 5,
+        + [pltpu.VMEM((64, 128), F32)] * 5
+        + [
+            pltpu.VMEM((64 * count, 1024), BF16),
+            pltpu.VMEM((devices, SENT, 128), BF16),
+            pltpu.VMEM((512, cells), BF16),
+            DMA((10,)),
+        ],
         cost_estimate=pl.CostEstimate(flops=10**10, bytes_accessed=8 << 20, transcendentals=0),
+        compiler_params=SMALL,
         name="learner",
-    )(lists, params, gathered, turned, u, targets)
+    )(lists, params, near(gathered), turned, far(u), targets)
 
     arrived = lax.all_to_all(send, "dev", 0, 0, tiled=True)
 
@@ -557,37 +618,44 @@
         score_kernel,
         out_shape=(
             jax.ShapeDtypeStruct((planes, count, CY, columns), F32),
-            jax.ShapeDtypeStruct((devices, devices * SENT), BF16),
+            pltpu.VMEM((devices, devices * SENT), BF16),
         ),
-        in_specs=[VMEM] * 5 + [ANY],
+        in_specs=[VMEM, HBM] + [VMEM] * 3 + [ANY],
         out_specs=(VMEM, VMEM),
         scratch_shapes=[
             PARAMS,
             pltpu.VMEM((3, 3, 64, 128), F32),
             pltpu.VMEM((512, 2304), BF16),
             pltpu.VMEM((3, planes + 2, CY * channels, cells + 256), BF16),
+            DMA((6,)),
         ],
         cost_estimate=pl.CostEstimate(flops=2 * 512 * 2304 * cells, bytes_accessed=8 << 20, transcendentals=0),
+        compiler_params=SMALL,
         name="score",
-    )(params, field, below, above, turned, vec)
+    )(params, far(field), below, above, turned, vec)
 
     final = pl.pallas_call(
         gradient_kernel,
         out_shape=jax.ShapeDtypeStruct((roles * devices * 8, 128), BF16),
-        in_specs=[VMEM] * 10,
+        in_specs=[VMEM] * 7 + [HBM] * 3,
         out_specs=VMEM,
         scratch_shapes=[
             PARAMS,
             pltpu.VMEM((512, cells), BF16),
             pltpu.VMEM((512, 768), F32),
             pltpu.VMEM((512, 128), F32),
+            pltpu.VMEM((512, cells), BF16),
+            pltpu.VMEM((64 * count, 1024), BF16),
+            pltpu.VMEM((3, planes, CY * channels, cells), BF16),
+            DMA((5,)),
         ],
         cost_estimate=pl.CostEstimate(flops=2 * 512 * 768 * cells, bytes_accessed=8 << 20, transcendentals=0),
+        compiler_params=SMALL,
         name="gradient",
     )(
         params,
-        arrived.reshape(devices * SENT, 128),
-        hot, mr, inverse, mine_row, g, u, field, vec,
+        near(arrived.reshape(devices * SENT, 128)),
+        near(hot), mr, inverse, mine_row, vec, far(g), far(u), far(field),
     )
     final = lax.all_to_all(
         final.reshape(roles * devices, 8, 128), ("role", "dev"), 0, 0, tiled=True
@@ -600,8 +668,9 @@
         ),
         in_specs=[VMEM],
         out_specs=(VMEM, VMEM),
+        compiler_params=SMALL,
         name="finish",
-    )(final)
+    )(near(final))
     return (scores.reshape(1, planes, height, columns), weight_grad, vector_grad)
 
 

time: 129 us -> 118 us (0.915)
  Pallas kernels: 47.1 us -> 38.2 us
  waiting for transfers between devices: 14.8 us -> 18.1 us
  local copies, waits for them, and re-layouts: 5.42 us -> 2.76 us
  blocking collectives: 17.1 us -> 14.7 us
    pallas_call x3, Pallas kernels: 22.8 us -> 17.8 us  [the longest x1 10.6 us: per_device(): pl.pallas_call(learner_kernel, out_shape=(pltpu.HBM((devices, SENT, 128),...]
    all_to_all x1, blocking collectives: 17.1 us -> 14.7 us  [per_device(): lax.all_to_all(final.reshape(roles * devices, 8, 128), ('role', 'dev'), 0...]
    all_to_all x1, waiting for transfers between devices: 3.48 us -> 5.72 us  [per_device(): arrived = lax.all_to_all(send, 'dev', 0, 0, tiled=True)]
    unnamed x15 -> x9, local copies, waits for them, and re-layouts: 3.52 us -> 1.31 us
  transfers between devices with their start and end apart: 5 -> 5, of which waited for: 2 -> 2; matrix products, arithmetic and copies ran while one was open for 4% -> 3% of each run, Pallas kernels for 27% -> 25%
where the time goes in v2:
time: 118 us; the launch traced here: 117 us
  Pallas kernels  38.2 us (32%)
  starting transfers between devices  36.9 us (31%)
  waiting for transfers between devices  18.1 us (15%)
  blocking collectives  14.7 us (12%)
  between operations  4.03 us (3%)
  local copies, waits for them, and re-layouts  2.76 us (2%)
  other arithmetic  2.53 us (2%)
    all_to_all x1, blocking collectives, per_device(): lax.all_to_all(final.reshape(roles * devices, 8, 128), ('role', 'dev'), 0...  14.7 us
    all_to_all x1, starting transfers between devices, per_device(): params = near(lax.all_to_all(rows, 'dev', 0, 0, tiled=True))  12.5 us
    all_to_all x1, waiting for transfers between devices, per_device(): gathered = lax.all_to_all(stats, 'dev', 0, 0, tiled=True)  12.4 us
    all_to_all x1, starting transfers between devices, per_device(): gathered = lax.all_to_all(stats, 'dev', 0, 0, tiled=True)  11.6 us
    pallas_call x1, Pallas kernels, per_device(): pl.pallas_call(score_kernel, out_shape=(jax.ShapeDtypeStruct((planes, cou...  11 us
    pallas_call x1, Pallas kernels, per_device(): pl.pallas_call(learner_kernel, out_shape=(pltpu.HBM((devices, SENT, 128),...  10.6 us
    pallas_call x1, Pallas kernels, per_device(): pl.pallas_call(gradient_kernel, out_shape=jax.ShapeDtypeStruct((roles * d...  8.02 us
    all_to_all x1, starting transfers between devices, per_device(): arrived = lax.all_to_all(send, 'dev', 0, 0, tiled=True)  7.31 us
  transfers between devices with their start and end apart: 5, of which 2 were waited for; matrix products, arithmetic and copies ran while one was open for 3% of the time, Pallas kernels for 25%

profile of v2, /device:TPU:1, one launch (start us, length us, event | category | flops | bytes accessed | tf_op | source)
XLA Modules:
  0.0 117.2 jit_solution(5822436933587540267)
XLA Ops:
  3.9 0.8 pad_add_fusion.row_ref
  4.7 0.7 pack.1
  5.4 12.5 %all-to-all-start = ((bf16[64,8,128]{2,1,0:T(8,128)(2,1)}), bf16[64,8,128]{2,1,0:T(8,128)(2,1)S(1)}, u32[]{:S(2)}, u32[]{:S(2)}) async-start(bf16[64,8,128]{2,1,0:T(8,128)(2,1)} %pack.1), calls=%async_computation | async-start | bytes 262144 | tf_op jit(solution)/shard_map/all_to_all | solution.py:525
  17.8 1.2 %copy-done.1 = bf16[1,32,2,64,128]{4,3,2,1,0:T(8,128)(2,1)S(1)} copy-done((bf16[1,32,2,64,128]{4,3,2,1,0:T(8,128)(2,1)S(1)}, bf16[1,32,2,64,128]{4,3,2,1,0:T(8,128)(2,1)}, u32[]{:S(2)}) %copy-start.1) | copy-done | bytes 1048600
  19.1 2.1 %prep.1.x_ref.x_in_ref = bf16[3,2,128,2048]{3,2,1,0:T(8,128)(2,1)S(1)} custom-call(bf16[32,2,64,128]{3,2,1,0:T(8,128)(2,1)S(1)} %bitcast.23), custom_call_target="tpu_custom_call" | custom-call | flops 10000000 | bytes 4194304 | tf_op jit(solution)/shard_map/prep/pallas_call | solution.py:531
  21.2 1.2 %slice_bitcast_fusion = (bf16[1,128,2048]{2,1,0:T(8,128)(2,1)}, bf16[1,128,2048]{2,1,0:T(8,128)(2,1)}) fusion(bf16[3,2,128,2048]{3,2,1,0:T(8,128)(2,1)S(1)} %prep.1.x_ref.x_in_ref), kind=kLoop, calls=%fused_computation | loop fusion | bytes 2097152 | tf_op jit(solution)/shard_map/slice | solution.py:582
  22.4 3.5 %collective-permute-start = (bf16[1,128,2048]{2,1,0:T(8,128)(2,1)}, bf16[1,128,2048]{2,1,0:T(8,128)(2,1)}, u32[]{:S(2)}, u32[]{:S(2)}) collective-permute-start(bf16[1,128,2048]{2,1,0:T(8,128)(2,1)} %get-tuple-element.30), channel_id=1, source_target_pairs={{0,1},{1,2},{2,3},{3,4},{4,5},{5,6},{6,7},{7,8},{8,9},{9,10},{10,1... | collective-permute-start | bytes 1572872 | tf_op jit(solution)/shard_map/ppermute | solution.py:581
  25.9 1.9 %collective-permute-start.1 = (bf16[1,128,2048]{2,1,0:T(8,128)(2,1)}, bf16[1,128,2048]{2,1,0:T(8,128)(2,1)}, u32[]{:S(2)}, u32[]{:S(2)}) collective-permute-start(bf16[1,128,2048]{2,1,0:T(8,128)(2,1)} %get-tuple-element.29), channel_id=1, source_target_pairs={{1,0},{2,1},{3,2},{4,3},{5,4},{6,5},{7,6},{8,7},{9,8},{10,9},{11,1... | collective-permute-start | bytes 1572872 | tf_op jit(solution)/shard_map/ppermute | solution.py:582
  28.0 5.1 %crop_conv.1 = (bf16[1024,1024]{1,0:T(8,128)(2,1)}, f32[64,16,128]{2,1,0:T(8,128)}) custom-call(bf16[64,8,128]{2,1,0:T(8,128)(2,1)S(1)} %all-to-all-done.w_ref, bf16[3,2,128,2048]{3,2,1,0:T(8,128)(2,1)S(1)} %prep.1.x_ref.x_in_ref), custom_call_target="tpu_custom_call" | custom-call | flops 1610612736 | bytes 8388608 | tf_op jit(solution)/shard_map/crop_conv/pallas_call | solution.py:546
  33.1 0.2 compare_reduce_fusion
  33.3 0.2 dynamic-slice_reduce_fusion
  33.5 11.6 %all-to-all-start.1 = ((f32[64,16,128]{2,1,0:T(8,128)}), f32[64,16,128]{2,1,0:T(8,128)S(1)}, u32[]{:S(2)}, u32[]{:S(2)}) async-start(f32[64,16,128]{2,1,0:T(8,128)} %get-tuple-element.16), calls=%async_computation.1 | async-start | bytes 1048576 | tf_op jit(solution)/shard_map/all_to_all | solution.py:578
  45.1 0.1 convert_reduce_fusion
  45.2 0.6 fusion.2
  45.9 0.1 select_reduce_fusion
  46.0 0.7 pad_add_fusion.1.cb_ref
  46.7 12.4 %all-to-all-done.1 = f32[64,16,128]{2,1,0:T(8,128)S(1)} async-done(((f32[64,16,128]{2,1,0:T(8,128)}), f32[64,16,128]{2,1,0:T(8,128)S(1)}, u32[]{:S(2)}, u32[]{:S(2)}) %all-to-all-start.1) | async-done | bytes 524320 | tf_op jit(solution)/shard_map/all_to_all | solution.py:578
  59.1 10.6 %learner.1 = (bf16[64,48,128]{2,1,0:T(8,128)(2,1)}, bf16[512,2048]{1,0:T(8,128)(2,1)}, f32[128,128]{1,0:T(8,128)S(1)}, f32[64,128]{1,0:T(8,128)S(1)}, f32[8,128]{1,0:T(8,128)S(1)}, /*index=5*/s32[8,128]{1,0:T(8,128)S(1)}) custom-call(s32[129]{0:T(256)S(1)} %pad_add_fusion.1.cb_ref, bf16[64,8,128]{2,1,0:T(8,128)(2,1)S(1)} %all-to-all-done.w_ref, ...), custom_call_target="tpu_custom_call" | custom-call | flops 10000000000 | bytes 8388608 | tf_op jit(solution)/shard_map/learner/pallas_call | solution.py:584
  69.6 7.3 %all-to-all-start.2 = ((bf16[64,48,128]{2,1,0:T(8,128)(2,1)}), bf16[64,48,128]{2,1,0:T(8,128)(2,1)S(1)}, u32[]{:S(2)}, u32[]{:S(2)}) async-start(bf16[64,48,128]{2,1,0:T(8,128)(2,1)} %get-tuple-element.21), calls=%async_computation.2 | async-start | bytes 1572864 | tf_op jit(solution)/shard_map/all_to_all | solution.py:615
  77.0 11.0 %score.1 = (f32[2,16,4,128]{3,2,1,0:T(4,128)}, bf16[64,3072]{1,0:T(8,128)(2,1)S(1)}) custom-call(bf16[64,8,128]{2,1,0:T(8,128)(2,1)S(1)} %all-to-all-done.w_ref, bf16[3,2,128,2048]{3,2,1,0:T(8,128)(2,1)} %copy-done, bf16[1,128,2048]{2,1,0:T(8,128)(2,1)} %collective-permute-done.below_ref, bf16[1,128,2048]{2,1,0:T(8,128)(2,1)} %collective-permute-done.1.above_ref, ...), custom_call_target="tpu_custom_call" | custom-call | flops 4831838208 | bytes 8388608 | tf_op jit(solution)/shard_map/score/pallas_call | solution.py:617
  88.0 5.7 %all-to-all-done.2 = bf16[64,48,128]{2,1,0:T(8,128)(2,1)S(1)} async-done(((bf16[64,48,128]{2,1,0:T(8,128)(2,1)}), bf16[64,48,128]{2,1,0:T(8,128)(2,1)S(1)}, u32[]{:S(2)}, u32[]{:S(2)}) %all-to-all-start.2) | async-done | bytes 786464 | tf_op jit(solution)/shard_map/all_to_all | solution.py:615
  93.7 8.0 %gradient.1 = bf16[1024,128]{1,0:T(8,128)(2,1)S(1)} custom-call(bf16[64,8,128]{2,1,0:T(8,128)(2,1)S(1)} %all-to-all-done.w_ref, bf16[3072,128]{1,0:T(8,128)(2,1)S(1)} %bitcast.21, bf16[64,3072]{1,0:T(8,128)(2,1)S(1)} %get-tuple-element.22.hot_ref, f32[128,128]{1,0:T(8,128)S(1)} %get-tuple-element.23.mr_ref, f32[8,128]{1,0:T(8,128)S(1)} %get-tuple-element.24.inv_ref, ...), custom_call_target="tpu_custom_call" | custom-call | flops 1610612736 | bytes 8388608 | tf_op jit(solution)/shard_map/gradient/pallas_call | solution.py:637
  101.8 14.7 %all_to_all.20.r_ref = bf16[128,8,128]{2,1,0:T(8,128)(2,1)S(1)} all-to-all(bf16[128,8,128]{2,1,0:T(8,128)(2,1)S(1)} %bitcast.22), channel_id=1, replica_groups=mesh['role'=2,'dev'=64] {'role','dev'}, dimensions={0} | all-to-all | bytes 524288 | tf_op jit(solution)/shard_map/all_to_all | solution.py:660
  116.5 0.7 finish.1
  (14 shorter events, 0.2 us)
Async XLA Ops:
  5.4 22.6 %all-to-all-start = ((bf16[64,8,128]{2,1,0:T(8,128)(2,1)}), bf16[64,8,128]{2,1,0:T(8,128)(2,1)S(1)}, u32[]{:S(2)}, u32[]{:S(2)}) async-start(bf16[64,8,128]{2,1,0:T(8,128)(2,1)} %pack.1), calls=%async_computation | async-start | bytes 262144 | tf_op jit(solution)/shard_map/all_to_all | solution.py:525
  17.8 1.2 %copy-start.1 = (bf16[1,32,2,64,128]{4,3,2,1,0:T(8,128)(2,1)S(1)}, bf16[1,32,2,64,128]{4,3,2,1,0:T(8,128)(2,1)}, u32[]{:S(2)}) copy-start(bf16[1,32,2,64,128]{4,3,2,1,0:T(8,128)(2,1)} %param.9) | copy-start | bytes 3145732
  19.1 8.8 %copy-start.3 = (s32[1,64,64]{2,1,0:T(8,128)S(1)}, s32[1,64,64]{2,1,0:T(8,128)}, u32[]{:S(2)}) copy-start(s32[1,64,64]{2,1,0:T(8,128)} %param.11) | copy-start | bytes 49156
  19.1 8.9 %copy-start.2 = (bf16[1,2,64,128]{3,2,1,0:T(8,128)(2,1)S(1)}, bf16[1,2,64,128]{3,2,1,0:T(8,128)(2,1)}, u32[]{:S(2)}) copy-start(bf16[1,2,64,128]{3,2,1,0:T(8,128)(2,1)} %param.10) | copy-start | bytes 98308
  21.2 11.9 %copy-start = (bf16[3,2,128,2048]{3,2,1,0:T(8,128)(2,1)}, bf16[3,2,128,2048]{3,2,1,0:T(8,128)(2,1)S(1)}, u32[]{:S(2)}) copy-start(bf16[3,2,128,2048]{3,2,1,0:T(8,128)(2,1)S(1)} %prep.1.x_ref.x_in_ref) | copy-start | bytes 9437188
  22.4 54.6 %collective-permute-start = (bf16[1,128,2048]{2,1,0:T(8,128)(2,1)}, bf16[1,128,2048]{2,1,0:T(8,128)(2,1)}, u32[]{:S(2)}, u32[]{:S(2)}) collective-permute-start(bf16[1,128,2048]{2,1,0:T(8,128)(2,1)} %get-tuple-element.30), channel_id=1, source_target_pairs={{0,1},{1,2},{2,3},{3,4},{4,5},{5,6},{6,7},{7,8},{8,9},{9,10},{10,1... | collective-permute-start | bytes 1572872 | tf_op jit(solution)/shard_map/ppermute | solution.py:581
  25.9 51.1 %collective-permute-start.1 = (bf16[1,128,2048]{2,1,0:T(8,128)(2,1)}, bf16[1,128,2048]{2,1,0:T(8,128)(2,1)}, u32[]{:S(2)}, u32[]{:S(2)}) collective-permute-start(bf16[1,128,2048]{2,1,0:T(8,128)(2,1)} %get-tuple-element.29), channel_id=1, source_target_pairs={{1,0},{2,1},{3,2},{4,3},{5,4},{6,5},{7,6},{8,7},{9,8},{10,9},{11,1... | collective-permute-start | bytes 1572872 | tf_op jit(solution)/shard_map/ppermute | solution.py:582
  33.5 25.6 %all-to-all-start.1 = ((f32[64,16,128]{2,1,0:T(8,128)}), f32[64,16,128]{2,1,0:T(8,128)S(1)}, u32[]{:S(2)}, u32[]{:S(2)}) async-start(f32[64,16,128]{2,1,0:T(8,128)} %get-tuple-element.16), calls=%async_computation.1 | async-start | bytes 1048576 | tf_op jit(solution)/shard_map/all_to_all | solution.py:578
  69.6 24.1 %all-to-all-start.2 = ((bf16[64,48,128]{2,1,0:T(8,128)(2,1)}), bf16[64,48,128]{2,1,0:T(8,128)(2,1)S(1)}, u32[]{:S(2)}, u32[]{:S(2)}) async-start(bf16[64,48,128]{2,1,0:T(8,128)(2,1)} %get-tuple-element.21), calls=%async_computation.2 | async-start | bytes 1572864 | tf_op jit(solution)/shard_map/all_to_all | solution.py:615

commit v3 on v2

--- a/solution.py
+++ b/solution.py
@@ -12,7 +12,6 @@
 F32 = jnp.float32
 BF16 = jnp.bfloat16
 PARAMS = pltpu.VMEM((512, 128), F32)
-ANY = pl.BlockSpec(memory_space=pl.ANY)
 VMEM = pl.BlockSpec(memory_space=pltpu.VMEM)
 SMALL = pltpu.CompilerParams(vmem_limit_bytes=20 << 20)
 HBM = pl.BlockSpec(memory_space=pltpu.HBM)
@@ -46,8 +45,8 @@
     return p_ref[pl.ds(k, 64, stride=8), :]
 
 
-def column(p_ref, k):
-    return chunk(p_ref, 6)[:, 96 + k : 97 + k]
+def column(v_ref, k):
+    return v_ref[:, k : k + 1]
 
 
 def fill_taps(p_ref, taps_ref):
@@ -73,11 +72,13 @@
     return v
 
 
-def pack_kernel(row_ref, out_ref):
+def pack_kernel(weight_ref, out_ref):
     sub = lax.broadcasted_iota(jnp.int32, (8, 128), 0)
     out = jnp.zeros((8, 128), F32)
-    for k in range(7):
-        out = jnp.where(sub == k, row_ref[:, 128 * k : 128 * k + 128], out)
+    for k in range(6):
+        out = jnp.where(sub == k, weight_ref[:, 128 * k : 128 * k + 128], out)
+    tail = jnp.concatenate([weight_ref[:, 768:864], jnp.zeros((1, 32), F32)], axis=1)
+    out = jnp.where(sub == 6, tail, out)
     out_ref[...] = jnp.broadcast_to(out.astype(BF16)[None], out_ref.shape)
 
 
@@ -88,7 +89,7 @@
     return left, v, right
 
 
-def prep_kernel(slab_ref, x_ref, wide_ref):
+def prep_kernel(slab_ref, x_ref, first_ref, last_ref, wide_ref, plane_ref, sem):
     channels, _, height, _ = slab_ref.shape
     wide_ref[...] = slab_ref[:, 0].astype(F32).reshape(channels * height, 128)
     for y in range(height):
@@ -97,10 +98,24 @@
         lanes = slice(128 * (y // CY), 128 * (y // CY) + 128)
         for c, w in enumerate(shifted(v)):
             x_ref[c, 0, rows, lanes] = w.astype(BF16)
+        plane_ref[pl.program_id(0), rows, lanes] = v.astype(BF16)
+    last = pl.num_programs(0) - 1
+    first_copy = pltpu.make_async_copy(plane_ref.at[0], first_ref.at[0], sem.at[0])
+    last_copy = pltpu.make_async_copy(plane_ref.at[last], last_ref.at[0], sem.at[1])
+
+    @pl.when(pl.program_id(0) == 0)
+    def _():
+        first_copy.start()
+
+    @pl.when(pl.program_id(0) == last)
+    def _():
+        last_copy.start()
+        first_copy.wait()
+        last_copy.wait()
 
 
 def crop_conv_kernel(
-    w_ref, x_ref, out_ref, stats_ref, p_ref, taps_ref, t_ref, s1_ref, m2_ref, u_ref, sem
+    gain_ref, shift_ref, head_ref, mean_ref, var_ref, w_ref, x_ref, out_ref, stats_ref, p_ref, taps_ref, t_ref, s1_ref, m2_ref, u_ref, sem
 ):
     load_params(w_ref, p_ref)
     fill_taps(p_ref, taps_ref)
@@ -161,7 +176,16 @@
     pairs = u_ref.shape[0] // 128
     lax.fori_loop(0, pairs - 1, step, 0)
     statistics(pairs - 1, u_ref[128 * (pairs - 1) :, :])
-    stats = jnp.concatenate([s1_ref[...], m2_ref[...]], axis=0).T[:16]
+    stat = jnp.concatenate([s1_ref[...], m2_ref[...]], axis=0).T[:16]
+    low = lanes[:16] < 64
+    high_term = stat.astype(BF16).astype(F32)
+    top = jnp.where(low, high_term, pltpu.roll(stat - high_term, 64, 1))
+    squares = jnp.where(low[:8], pltpu.roll(stat, 64, 1)[:8], stat[8:])
+    sub = lax.broadcasted_iota(jnp.int32, (8, 128), 0)
+    tail = jnp.zeros((8, 128), F32)
+    for k, ref in enumerate((gain_ref, shift_ref, head_ref, mean_ref, var_ref)):
+        tail = jnp.where((sub == 0) & (lanes[:8] == k), ref[0], tail)
+    stats = jnp.concatenate([top, squares, tail], axis=0).astype(BF16)
 
     def spread(s, _):
         stats_ref[s] = stats
@@ -173,7 +197,7 @@
 
 
 def score_kernel(
-    w_ref, x_ref, below_ref, above_ref, cbt_ref, _, out_ref, hot_ref, p_ref, taps_ref, t_ref, f_ref, sem
+    w_ref, x_ref, below_ref, above_ref, cbt_ref, v_ref, out_ref, hot_ref, p_ref, taps_ref, t_ref, f_ref, sem
 ):
     count = x_ref.shape[3] // 128
     arrive = []
@@ -226,7 +250,7 @@
                     col = 1536 + 128 * (2 * c + k)
                     v = edges[2 * k] + edges[2 * k + 1]
                     t_ref[row, col : col + 128] = v.astype(BF16)
-    gain, shift, head, mean, var = (column(p_ref, k) for k in range(5))
+    gain, shift, head, mean, var = (column(v_ref, k) for k in range(5))
     alpha = gain * lax.rsqrt(var + EPS)
     beta = shift - mean * alpha
     alpha = jnp.broadcast_to(alpha, (64, 128))
@@ -283,17 +307,20 @@
 
 
 def learner_kernel(
-    cb_ref, w_ref, r_ref, cbt_ref, u_in_ref, lab_ref,
-    send_out_ref, g_out_ref, mr_ref, vec_ref, inv_ref, row_ref,
+    cb_ref, r_ref, table_ref, u_in_ref, given_ref,
+    send_out_ref, g_out_ref, mr_ref, vec_ref, inv_ref, row_ref, v_ref, cbt_ref,
     p_ref, acc_ref, part_ref, coef_ref, scale_ref, al_ref, be_ref, hd_ref, r0_ref, ru_ref,
-    u_ref, send_ref, g_ref, sem,
+    u_ref, send_ref, g_ref, lab_ref, sem,
 ):
     arrive = pltpu.make_async_copy(u_in_ref, u_ref, sem.at[0])
     arrive.start()
-    load_params(w_ref, p_ref)
+    cbt_ref[...] = table_ref[...].astype(F32).T
+    given = given_ref[...].astype(F32)
+    for b in range(lab_ref.shape[0]):
+        lab_ref[b] = jnp.concatenate([given[z, CY * b : CY * b + CY] for z in range(2)], axis=0)
     lanes = lane_iota()
     learners, sources = cbt_ref.shape
-    entries = r_ref.shape[0]
+    entries = sources * 16
     lane = lax.broadcasted_iota(jnp.int32, (sources, entries), 1)
     source = lax.broadcasted_iota(jnp.int32, (sources, entries), 0)
     expand = jnp.where(lane // 16 == source, 1.0, 0.0).astype(BF16)
@@ -301,12 +328,19 @@
     which = lax.broadcasted_iota(jnp.int32, (learners, entries), 1) % 16
     onehot = jnp.where(wanted == which.astype(F32), 1.0, 0.0).astype(BF16)
     number = jnp.sum(jnp.where(cbt_ref[...] >= 0, 1.0, 0.0), axis=1, keepdims=True)
-    r = r_ref[...]
+    wide = r_ref[...].astype(F32)
+    low_half = lax.broadcasted_iota(jnp.int32, (entries, 128), 1) < 64
+    top = wide[:, :16].reshape(entries, 128)
+    squares = wide[:, 16:24]
+    swapped = pltpu.roll(squares.reshape(sources * 8, 128), 64, 1).reshape(sources, 8, 128)
+    squares = jnp.concatenate([swapped, squares], axis=1).reshape(entries, 128)
+    r = jnp.where(low_half, top + pltpu.roll(top, 64, 1), squares)
+    p_ref[...] = wide[:, 24:32].reshape(sources * 8, 128)
+    v_ref[...] = p_ref[pl.ds(0, sources, stride=8), :]
     means = r * (1.0 / 1024)
     centre = jnp.mean(means, axis=0, keepdims=True)
     d = means - centre
     rolled = pltpu.roll(d, 64, 1)
-    low_half = lax.broadcasted_iota(jnp.int32, (entries, 128), 1) < 64
     v = jnp.where(low_half, d, means + rolled * rolled)
     p = exact_dot(onehot, v) / number
     first = jnp.where(lanes < 64, p, 0.0)
@@ -320,7 +354,7 @@
     inverse = jnp.concatenate([inverse, jnp.zeros((128 - learners, 128), F32)], axis=0).T
     inv_ref[...] = inverse[:8]
     row_ref[...] = jnp.full((8, 128), -1, jnp.int32)
-    gain, shift, head = (jnp.broadcast_to(column(p_ref, k), (64, 128)) for k in range(3))
+    gain, shift, head = (jnp.broadcast_to(column(v_ref, k), (64, 128)) for k in range(3))
     alpha = gain * both_t[64:]
     al_ref[...] = alpha
     be_ref[...] = shift - alpha * both_t[:64]
@@ -355,7 +389,6 @@
     def learner(k, e):
         t = cb_ref[jnp.minimum(k, live - 1)]
         b = cb_ref[learners + t]
-        at = pl.multiple_of(b * 128, 128)
         row = pl.multiple_of(b * 64, 64)
         row_ref[...] = jnp.where(lanes[:8] == t, b, row_ref[...])
         al, be, c1 = (coef_ref[3 * e + n] for n in range(3))
@@ -371,7 +404,7 @@
             m = jnp.where(h > 0, res, 0.0)
             r0 = r0 + m
             rh = rh + h * res
-            acc_ref[64 * j : 64 * j + 64, pl.ds(at, 128)] += c1 * m
+            acc_ref[pl.ds(row, 64), 128 * j : 128 * j + 128] += c1 * m
         part_ref[2 * e] = r0
         part_ref[2 * e + 1] = rh
 
@@ -404,7 +437,7 @@
     send.start()
     leaves = []
     for j in range(8):
-        rows = slice(64 * j, 64 * j + 64)
+        rows = slice(128 * j, 128 * j + 128)
         g_ref[rows, :] = acc_ref[rows, :].astype(BF16)
         leaves.append(pltpu.make_async_copy(g_ref.at[rows], g_out_ref.at[rows], sem.at[2 + j]))
         leaves[j].start()
@@ -420,21 +453,21 @@
 
 
 def gradient_kernel(
-    w_ref, r_ref, hot_ref, mr_ref, inv_ref, cb_ref, vec_ref, g_in_ref, u_in_ref, x_in_ref,
-    out_ref, p_ref, full_ref, dt_ref, row_ref, g_ref, u_ref, x_ref, sem,
+    v_ref, r_ref, hot_ref, mr_ref, inv_ref, cb_ref, vec_ref, g_in_ref, u_in_ref, x_in_ref,
+    out_ref, full_ref, dt_ref, row_ref, g_ref, u_ref, x_ref, sem,
 ):
-    arrive = [
-        pltpu.make_async_copy(g_in_ref, g_ref, sem.at[0]),
-        pltpu.make_async_copy(u_in_ref, u_ref, sem.at[1]),
-    ]
-    arrive += [pltpu.make_async_copy(x_in_ref.at[c], x_ref.at[c], sem.at[2 + c]) for c in range(3)]
+    arrive = []
+    for q in range(4):
+        rows = pl.ds(256 * q, 256)
+        arrive.append(pltpu.make_async_copy(g_in_ref.at[rows], g_ref.at[rows], sem.at[2 * q]))
+        arrive.append(pltpu.make_async_copy(u_in_ref.at[rows], u_ref.at[rows], sem.at[2 * q + 1]))
+    arrive += [pltpu.make_async_copy(x_in_ref.at[c], x_ref.at[c], sem.at[8 + c]) for c in range(3)]
     for copy in arrive:
         copy.start()
-    load_params(w_ref, p_ref)
     learners = hot_ref.shape[0]
     total = jnp.dot(hot_ref[...], r_ref[...], preferred_element_type=F32)
     total = jnp.concatenate([total, jnp.zeros((128 - learners, 128), F32)], axis=0).T
-    gain, head = (jnp.broadcast_to(column(p_ref, k), (64, 128)) for k in (0, 2))
+    gain, head = (jnp.broadcast_to(column(v_ref, k), (64, 128)) for k in (0, 2))
     factor = gain * head * inv_ref[0:1, :]
     first = factor * total[:64]
     second = factor * total[64:]
@@ -452,16 +485,17 @@
         f = jnp.broadcast_to(jnp.sum(jnp.where(here, slope, 0.0), axis=1, keepdims=True), (64, 128))
         for j in range(8):
             rows = slice(64 * j, 64 * j + 64)
-            v = g_ref[rows, pl.ds(at, 128)].astype(F32) - e
+            v = g_ref[pl.ds(row64, 64), 128 * j : 128 * j + 128].astype(F32) - e
             v = v - f * u_ref[pl.ds(row64, 64), 128 * j : 128 * j + 128].astype(F32)
             full_ref[rows, pl.ds(at, 128)] = v.astype(BF16)
         return 0
 
-    arrive[0].wait()
-    arrive[1].wait()
-    lax.fori_loop(0, 16, block, 0)
+    for q in range(4):
+        arrive[2 * q].wait()
+        arrive[2 * q + 1].wait()
+        lax.fori_loop(4 * q, 4 * q + 4, block, 0, unroll=2)
     for c in range(3):
-        arrive[2 + c].wait()
+        arrive[8 + c].wait()
         dt_ref[:, 256 * c : 256 * c + 256] = lax.dot_general(
             full_ref[...],
             jnp.concatenate([x_ref[c, 0], x_ref[c, 1]], axis=0),
@@ -511,9 +545,6 @@
 def per_device(features, labels, crop_block, weight, gain, shift, head, run_mean, run_var):
     devices = lax.axis_size("dev")
     roles = lax.axis_size("role")
-    row = jnp.pad(weight, ((0, 0), (0, 896 - 864)))
-    vectors = jnp.concatenate([gain, shift, head, run_mean, run_var])
-    row = row + jnp.pad(vectors[None], ((0, 0), (864, 27)))
     rows = pl.pallas_call(
         pack_kernel,
         out_shape=jax.ShapeDtypeStruct((devices, 8, 128), BF16),
@@ -521,35 +552,45 @@
         out_specs=VMEM,
         compiler_params=SMALL,
         name="pack",
-    )(row)
+    )(far(weight))
     params = near(lax.all_to_all(rows, "dev", 0, 0, tiled=True))
 
     slab = features[0]
     channels, planes, height, columns = slab.shape
     count = height // CY
     cells = count * columns
-    field = pl.pallas_call(
+    field, first, last = pl.pallas_call(
         prep_kernel,
-        out_shape=pltpu.VMEM((3, planes, CY * channels, cells), BF16),
+        out_shape=(
+            pltpu.VMEM((3, planes, CY * channels, cells), BF16),
+            pltpu.HBM((1, CY * channels, cells), BF16),
+            pltpu.HBM((1, CY * channels, cells), BF16),
+        ),
         grid=(planes,),
         in_specs=[pl.BlockSpec((channels, 1, height, columns), lambda z: (0, z, 0, 0))],
-        out_specs=pl.BlockSpec((3, 1, CY * channels, cells), lambda z: (0, z, 0, 0)),
-        scratch_shapes=[pltpu.VMEM((channels * height, columns), F32)],
+        out_specs=(
+            pl.BlockSpec((3, 1, CY * channels, cells), lambda z: (0, z, 0, 0)),
+            HBM,
+            HBM,
+        ),
+        scratch_shapes=[
+            pltpu.VMEM((channels * height, columns), F32),
+            pltpu.VMEM((planes, CY * channels, cells), BF16),
+            DMA((2,)),
+        ],
         cost_estimate=pl.CostEstimate(flops=10**7, bytes_accessed=4 << 20, transcendentals=0),
         compiler_params=SMALL,
         name="prep",
-    )(slab)
-
-    targets = labels[0].reshape(planes, count, CY, columns).transpose(1, 0, 2, 3)
-    targets = targets.reshape(count, planes * CY, columns).astype(F32)
-
+    )(far(slab))
+
+    *vectors, _ = lax.optimization_barrier((gain, shift, head, run_mean, run_var, field))
     u, stats = pl.pallas_call(
         crop_conv_kernel,
         out_shape=(
             pltpu.HBM((64 * count, 1024), BF16),
-            pltpu.HBM((devices, count, 128), F32),
+            pltpu.HBM((devices, 32, 128), BF16),
         ),
-        in_specs=[VMEM] * 2,
+        in_specs=[SMEM] * 5 + [VMEM] * 2,
         out_specs=(HBM, VMEM),
         scratch_shapes=[
             PARAMS,
@@ -563,7 +604,7 @@
         cost_estimate=pl.CostEstimate(flops=2 * 512 * 768 * cells, bytes_accessed=8 << 20, transcendentals=0),
         compiler_params=SMALL,
         name="crop_conv",
-    )(params, near(field))
+    )(*vectors, params, near(field))
 
     table, _ = lax.optimization_barrier((crop_block[0], stats))
     own_index = lax.axis_index("dev")
@@ -574,28 +615,27 @@
     at = live[None, :] & (before[None, :] == places[:, None])
     order = jnp.sum(jnp.where(at, places[None, :], 0), axis=1)
     lists = jnp.concatenate([order, mine, jnp.sum(live.astype(jnp.int32))[None]]).astype(jnp.int32)
-    turned = table.T.astype(F32)
     gathered = lax.all_to_all(stats, "dev", 0, 0, tiled=True)
-    gathered = gathered.reshape(devices * count, 128)
-    plane = field[1]
-    below = lax.ppermute(plane[-1:], "dev", [(i, i + 1) for i in range(devices - 1)])
-    above = lax.ppermute(plane[:1], "dev", [(i + 1, i) for i in range(devices - 1)])
-
-    send, g, mr, vec, inverse, mine_row = pl.pallas_call(
+    below = lax.ppermute(last, "dev", [(i, i + 1) for i in range(devices - 1)])
+    above = lax.ppermute(first, "dev", [(i + 1, i) for i in range(devices - 1)])
+
+    send, g, mr, vec, inverse, mine_row, values, turned = pl.pallas_call(
         learner_kernel,
         out_shape=(
             pltpu.HBM((devices, SENT, 128), BF16),
-            pltpu.HBM((512, cells), BF16),
+            pltpu.HBM((64 * count, 1024), BF16),
             jax.ShapeDtypeStruct((128, 128), F32),
             jax.ShapeDtypeStruct((64, 128), F32),
             jax.ShapeDtypeStruct((8, 128), F32),
             jax.ShapeDtypeStruct((8, 128), jnp.int32),
+            jax.ShapeDtypeStruct((64, 128), F32),
+            jax.ShapeDtypeStruct((devices, devices), F32),
         ),
-        in_specs=[SMEM] + [VMEM] * 3 + [HBM, VMEM],
-        out_specs=(HBM, HBM) + (VMEM,) * 4,
+        in_specs=[SMEM] + [VMEM] * 2 + [HBM, VMEM],
+        out_specs=(HBM, HBM) + (VMEM,) * 6,
         scratch_shapes=[
             PARAMS,
-            pltpu.VMEM((512, cells), F32),
+            pltpu.VMEM((64 * count, 1024), F32),
             pltpu.VMEM((4, 64, 128), F32),
             pltpu.VMEM((6, 64, 128), F32),
             pltpu.VMEM((2, 8, 128), F32),
@@ -604,13 +644,14 @@
         + [
             pltpu.VMEM((64 * count, 1024), BF16),
             pltpu.VMEM((devices, SENT, 128), BF16),
-            pltpu.VMEM((512, cells), BF16),
+            pltpu.VMEM((64 * count, 1024), BF16),
+            pltpu.VMEM((count, planes * CY, columns), F32),
             DMA((10,)),
         ],
         cost_estimate=pl.CostEstimate(flops=10**10, bytes_accessed=8 << 20, transcendentals=0),
         compiler_params=SMALL,
         name="learner",
-    )(lists, params, near(gathered), turned, far(u), targets)
+    )(lists, near(gathered), table, far(u), labels[0])
 
     arrived = lax.all_to_all(send, "dev", 0, 0, tiled=True)
 
@@ -620,7 +661,7 @@
             jax.ShapeDtypeStruct((planes, count, CY, columns), F32),
             pltpu.VMEM((devices, devices * SENT), BF16),
         ),
-        in_specs=[VMEM, HBM] + [VMEM] * 3 + [ANY],
+        in_specs=[VMEM, HBM] + [VMEM] * 4,
         out_specs=(VMEM, VMEM),
         scratch_shapes=[
             PARAMS,
@@ -632,7 +673,7 @@
         cost_estimate=pl.CostEstimate(flops=2 * 512 * 2304 * cells, bytes_accessed=8 << 20, transcendentals=0),
         compiler_params=SMALL,
         name="score",
-    )(params, far(field), below, above, turned, vec)
+    )(params, far(field), below, above, turned, values)
 
     final = pl.pallas_call(
         gradient_kernel,
@@ -640,20 +681,19 @@
         in_specs=[VMEM] * 7 + [HBM] * 3,
         out_specs=VMEM,
         scratch_shapes=[
-            PARAMS,
             pltpu.VMEM((512, cells), BF16),
             pltpu.VMEM((512, 768), F32),
             pltpu.VMEM((512, 128), F32),
-            pltpu.VMEM((512, cells), BF16),
+            pltpu.VMEM((64 * count, 1024), BF16),
             pltpu.VMEM((64 * count, 1024), BF16),
             pltpu.VMEM((3, planes, CY * channels, cells), BF16),
-            DMA((5,)),
+            DMA((11,)),
         ],
         cost_estimate=pl.CostEstimate(flops=2 * 512 * 768 * cells, bytes_accessed=8 << 20, transcendentals=0),
         compiler_params=SMALL,
         name="gradient",
     )(
-        params,
+        values,
         near(arrived.reshape(devices * SENT, 128)),
         near(hot), mr, inverse, mine_row, vec, far(g), far(u), far(field),
     )

time: 118 us -> 114 us (0.966)
  local copies, waits for them, and re-layouts: 2.76 us -> 0.02 us
    pallas_call x1, Pallas kernels: 2.1 us -> 4.06 us  [per_device(): pl.pallas_call(prep_kernel, out_shape=(pltpu.VMEM((3, planes, CY * channe...]
    pallas_call x1, Pallas kernels: 8.02 us -> 6.46 us  [per_device(): pl.pallas_call(gradient_kernel, out_shape=jax.ShapeDtypeStruct((roles * d...]
    unnamed x9 -> x6, local copies, waits for them, and re-layouts: 1.31 us -> 0.02 us
    slice x1 -> x0, local copies, waits for them, and re-layouts: 1.18 us -> none  [per_device(): plane[:1]]
  transfers between devices with their start and end apart: 5 -> 5, of which waited for: 2 -> 2; matrix products, arithmetic and copies ran while one was open for 3% -> 1% of each run, Pallas kernels for 25% -> 26%
where the time goes in v3:
time: 114 us
  Pallas kernels  38.6 us (34%)
  starting transfers between devices  36.6 us (32%)
  waiting for transfers between devices  18.1 us (16%)
  blocking collectives  14.7 us (13%)
  between operations  4.03 us (4%)
  other arithmetic  1.61 us (1%)
    all_to_all x1, blocking collectives, per_device(): lax.all_to_all(final.reshape(roles * devices, 8, 128), ('role', 'dev'), 0...  14.7 us
    all_to_all x1, starting transfers between devices, per_device(): params = near(lax.all_to_all(rows, 'dev', 0, 0, tiled=True))  12.5 us
    all_to_all x1, waiting for transfers between devices, per_device(): gathered = lax.all_to_all(stats, 'dev', 0, 0, tiled=True)  12.3 us
    all_to_all x1, starting transfers between devices, per_device(): gathered = lax.all_to_all(stats, 'dev', 0, 0, tiled=True)  11.6 us
    pallas_call x1, Pallas kernels, per_device(): pl.pallas_call(score_kernel, out_shape=(jax.ShapeDtypeStruct((planes, cou...  11 us
    pallas_call x1, Pallas kernels, per_device(): pl.pallas_call(learner_kernel, out_shape=(pltpu.HBM((devices, SENT, 128),...  9.89 us
    all_to_all x1, starting transfers between devices, per_device(): arrived = lax.all_to_all(send, 'dev', 0, 0, tiled=True)  7 us
    pallas_call x1, Pallas kernels, per_device(): pl.pallas_call(gradient_kernel, out_shape=jax.ShapeDtypeStruct((roles * d...  6.46 us
  transfers between devices with their start and end apart: 5, of which 2 were waited for; matrix products, arithmetic and copies ran while one was open for 1% of the time, Pallas kernels for 26%

profile of v3, /device:TPU:1, one launch (start us, length us, event | category | flops | bytes accessed | tf_op | source)
XLA Modules:
  0.0 113.6 jit_solution(18149610094422384780)
XLA Ops:
  0.6 1.3 %pack.1 = bf16[64,8,128]{2,1,0:T(8,128)(2,1)} custom-call(f32[1,864]{1,0:T(1,128)} %weight_ref.1), custom_call_target="tpu_custom_call" | custom-call | tf_op jit(solution)/shard_map/pack/pallas_call | solution.py:548
  2.0 12.5 %all-to-all-start = ((bf16[64,8,128]{2,1,0:T(8,128)(2,1)}), bf16[64,8,128]{2,1,0:T(8,128)(2,1)S(1)}, u32[]{:S(2)}, u32[]{:S(2)}) async-start(bf16[64,8,128]{2,1,0:T(8,128)(2,1)} %pack.1), calls=%async_computation | async-start | bytes 262144 | tf_op jit(solution)/shard_map/all_to_all | solution.py:556
  14.4 4.1 %prep.1 = (bf16[3,2,128,2048]{3,2,1,0:T(8,128)(2,1)S(1)}, bf16[1,128,2048]{2,1,0:T(8,128)(2,1)}, bf16[1,128,2048]{2,1,0:T(8,128)(2,1)}) custom-call(bf16[32,2,64,128]{3,2,1,0:T(8,128)(2,1)} %bitcast.18), custom_call_target="tpu_custom_call" | custom-call | flops 10000000 | bytes 4194304 | tf_op jit(solution)/shard_map/prep/pallas_call | solution.py:562
  18.5 3.5 %collective-permute-start = (bf16[1,128,2048]{2,1,0:T(8,128)(2,1)}, bf16[1,128,2048]{2,1,0:T(8,128)(2,1)}, u32[]{:S(2)}, u32[]{:S(2)}) collective-permute-start(bf16[1,128,2048]{2,1,0:T(8,128)(2,1)} %get-tuple-element.27), channel_id=1, source_target_pairs={{0,1},{1,2},{2,3},{3,4},{4,5},{5,6},{6,7},{7,8},{8,9},{9,10},{10,1... | collective-permute-start | bytes 1572872 | tf_op jit(solution)/shard_map/ppermute | solution.py:619
  22.1 1.9 %collective-permute-start.1 = (bf16[1,128,2048]{2,1,0:T(8,128)(2,1)}, bf16[1,128,2048]{2,1,0:T(8,128)(2,1)}, u32[]{:S(2)}, u32[]{:S(2)}) collective-permute-start(bf16[1,128,2048]{2,1,0:T(8,128)(2,1)} %get-tuple-element.28), channel_id=1, source_target_pairs={{1,0},{2,1},{3,2},{4,3},{5,4},{6,5},{7,6},{8,7},{9,8},{10,9},{11,1... | collective-permute-start | bytes 1572872 | tf_op jit(solution)/shard_map/ppermute | solution.py:620
  27.2 0.0 all-to-all-done.w_ref
  27.2 0.0 copy-start.1
  27.3 0.0 copy-start.2
  27.3 5.1 %crop_conv.1 = (bf16[1024,1024]{1,0:T(8,128)(2,1)}, bf16[64,32,128]{2,1,0:T(8,128)(2,1)}) custom-call(f32[1]{0:T(128)S(6)} %copy.12.gain_ref, f32[1]{0:T(128)S(6)} %copy.13.shift_ref, f32[1]{0:T(128)S(6)} %copy.14.head_ref, f32[1]{0:T(128)S(6)} %copy.15.mean_ref, f32[1]{0:T(128)S(6)} %copy.16.var_ref, bf16[64,8,128]{2,1,0:T(8,128)(2,1)S(1)} %all-to-all-done.w_ref, ...), custom_call_target="tpu_custom_call" | custom-call | flops 1610612736 | bytes 8388608 | tf_op jit(solution)/shard_map/crop_conv/pallas_call | solution.py:587
  32.4 11.6 %all-to-all-start.1 = ((bf16[64,32,128]{2,1,0:T(8,128)(2,1)}), bf16[64,32,128]{2,1,0:T(8,128)(2,1)S(1)}, u32[]{:S(2)}, u32[]{:S(2)}) async-start(bf16[64,32,128]{2,1,0:T(8,128)(2,1)} %get-tuple-element.34), calls=%async_computation.1 | async-start | bytes 1048576 | tf_op jit(solution)/shard_map/all_to_all | solution.py:618
  44.1 0.6 fusion.2
  44.7 0.1 convert_reduce_fusion
  44.9 0.1 select_reduce_fusion
  45.0 0.7 pad_add_fusion.cb_ref
  45.7 12.3 %all-to-all-done.1.r_ref = bf16[64,32,128]{2,1,0:T(8,128)(2,1)S(1)} async-done(((bf16[64,32,128]{2,1,0:T(8,128)(2,1)}), bf16[64,32,128]{2,1,0:T(8,128)(2,1)S(1)}, u32[]{:S(2)}, u32[]{:S(2)}) %all-to-all-start.1) | async-done | bytes 524320 | tf_op jit(solution)/shard_map/all_to_all | solution.py:618
  58.0 9.9 %learner.1 = (bf16[64,48,128]{2,1,0:T(8,128)(2,1)}, bf16[1024,1024]{1,0:T(8,128)(2,1)}, f32[128,128]{1,0:T(8,128)S(1)}, f32[64,128]{1,0:T(8,128)S(1)}, f32[8,128...) custom-call(s32[129]{0:T(256)S(1)} %pad_add_fusion.cb_ref, ...), custom_call_target="tpu_custom_call" | custom-call | flops 10000000000 | bytes 8388608 | tf_op jit(solution)/shard_map/learner/pallas_call | solution.py:622
  67.9 7.0 %all-to-all-start.2 = ((bf16[64,48,128]{2,1,0:T(8,128)(2,1)}), bf16[64,48,128]{2,1,0:T(8,128)(2,1)S(1)}, u32[]{:S(2)}, u32[]{:S(2)}) async-start(bf16[64,48,128]{2,1,0:T(8,128)(2,1)} %get-tuple-element.40), calls=%async_computation.2 | async-start | bytes 1572864 | tf_op jit(solution)/shard_map/all_to_all | solution.py:656
  74.9 0.0 collective-permute-done.below_ref
  74.9 0.0 collective-permute-done.1.above_ref
  75.0 11.0 %score.1 = (f32[2,16,4,128]{3,2,1,0:T(4,128)}, bf16[64,3072]{1,0:T(8,128)(2,1)S(1)}) custom-call(bf16[64,8,128]{2,1,0:T(8,128)(2,1)S(1)} %all-to-all-done.w_ref, bf16[3,2,128,2048]{3,2,1,0:T(8,128)(2,1)} %copy-done, bf16[1,128,2048]{2,1,0:T(8,128)(2,1)} %collective-permute-done.below_ref, bf16[1,128,2048]{2,1,0:T(8,128)(2,1)} %collective-permute-done.1.above_ref, ...), custom_call_target="tpu_custom_call" | custom-call | flops 4831838208 | bytes 8388608 | tf_op jit(solution)/shard_map/score/pallas_call | solution.py:658
  86.0 5.7 %all-to-all-done.2 = bf16[64,48,128]{2,1,0:T(8,128)(2,1)S(1)} async-done(((bf16[64,48,128]{2,1,0:T(8,128)(2,1)}), bf16[64,48,128]{2,1,0:T(8,128)(2,1)S(1)}, u32[]{:S(2)}, u32[]{:S(2)}) %all-to-all-start.2) | async-done | bytes 786464 | tf_op jit(solution)/shard_map/all_to_all | solution.py:656
  91.7 6.5 %gradient.1 = bf16[1024,128]{1,0:T(8,128)(2,1)S(1)} custom-call(f32[64,128]{1,0:T(8,128)S(1)} %get-tuple-element.38.v_ref, bf16[3072,128]{1,0:T(8,128)(2,1)S(1)} %bitcast.12, bf16[64,3072]{1,0:T(8,128)(2,1)S(1)} %get-tuple-element.41.hot_ref, f32[128,128]{1,0:T(8,128)S(1)} %get-tuple-element.42.mr_ref, f32[8,128]{1,0:T(8,128)S(1)} %get-tuple-element.43.inv_ref, ...), custom_call_target="tpu_custom_call" | custom-call | flops 1610612736 | bytes 8388608 | tf_op jit(solution)/shard_map/gradient/pallas_call | solution.py:678
  98.2 14.7 %all_to_all.20.r_ref = bf16[128,8,128]{2,1,0:T(8,128)(2,1)S(1)} all-to-all(bf16[128,8,128]{2,1,0:T(8,128)(2,1)S(1)} %bitcast.13), channel_id=1, replica_groups=mesh['role'=2,'dev'=64] {'role','dev'}, dimensions={0} | all-to-all | bytes 524288 | tf_op jit(solution)/shard_map/all_to_all | solution.py:700
  112.9 0.7 finish.1
  (5 shorter events, 0.0 us)
Async XLA Ops:
  2.0 25.3 %all-to-all-start = ((bf16[64,8,128]{2,1,0:T(8,128)(2,1)}), bf16[64,8,128]{2,1,0:T(8,128)(2,1)S(1)}, u32[]{:S(2)}, u32[]{:S(2)}) async-start(bf16[64,8,128]{2,1,0:T(8,128)(2,1)} %pack.1), calls=%async_computation | async-start | bytes 262144 | tf_op jit(solution)/shard_map/all_to_all | solution.py:556
  18.5 13.9 %copy-start = (bf16[3,2,128,2048]{3,2,1,0:T(8,128)(2,1)}, bf16[3,2,128,2048]{3,2,1,0:T(8,128)(2,1)S(1)}, u32[]{:S(2)}) copy-start(bf16[3,2,128,2048]{3,2,1,0:T(8,128)(2,1)S(1)} %get-tuple-element.26.x_ref.x_in_ref) | copy-start | bytes 9437188
  18.5 56.4 %collective-permute-start = (bf16[1,128,2048]{2,1,0:T(8,128)(2,1)}, bf16[1,128,2048]{2,1,0:T(8,128)(2,1)}, u32[]{:S(2)}, u32[]{:S(2)}) collective-permute-start(bf16[1,128,2048]{2,1,0:T(8,128)(2,1)} %get-tuple-element.27), channel_id=1, source_target_pairs={{0,1},{1,2},{2,3},{3,4},{4,5},{5,6},{6,7},{7,8},{8,9},{9,10},{10,1... | collective-permute-start | bytes 1572872 | tf_op jit(solution)/shard_map/ppermute | solution.py:619
  22.1 52.9 %collective-permute-start.1 = (bf16[1,128,2048]{2,1,0:T(8,128)(2,1)}, bf16[1,128,2048]{2,1,0:T(8,128)(2,1)}, u32[]{:S(2)}, u32[]{:S(2)}) collective-permute-start(bf16[1,128,2048]{2,1,0:T(8,128)(2,1)} %get-tuple-element.28), channel_id=1, source_target_pairs={{1,0},{2,1},{3,2},{4,3},{5,4},{6,5},{7,6},{8,7},{9,8},{10,9},{11,1... | collective-permute-start | bytes 1572872 | tf_op jit(solution)/shard_map/ppermute | solution.py:620
  27.2 16.8 %copy-start.1 = (s32[1,64,64]{2,1,0:T(8,128)S(1)}, s32[1,64,64]{2,1,0:T(8,128)}, u32[]{:S(2)}) copy-start(s32[1,64,64]{2,1,0:T(8,128)} %param.11) | copy-start | bytes 49156
  27.3 30.8 %copy-start.2 = (bf16[1,2,64,128]{3,2,1,0:T(8,128)(2,1)S(1)}, bf16[1,2,64,128]{3,2,1,0:T(8,128)(2,1)}, u32[]{:S(2)}) copy-start(bf16[1,2,64,128]{3,2,1,0:T(8,128)(2,1)} %param.10) | copy-start | bytes 98308
  32.4 25.6 %all-to-all-start.1 = ((bf16[64,32,128]{2,1,0:T(8,128)(2,1)}), bf16[64,32,128]{2,1,0:T(8,128)(2,1)S(1)}, u32[]{:S(2)}, u32[]{:S(2)}) async-start(bf16[64,32,128]{2,1,0:T(8,128)(2,1)} %get-tuple-element.34), calls=%async_computation.1 | async-start | bytes 1048576 | tf_op jit(solution)/shard_map/all_to_all | solution.py:618
  67.9 23.8 %all-to-all-start.2 = ((bf16[64,48,128]{2,1,0:T(8,128)(2,1)}), bf16[64,48,128]{2,1,0:T(8,128)(2,1)S(1)}, u32[]{:S(2)}, u32[]{:S(2)}) async-start(bf16[64,48,128]{2,1,0:T(8,128)(2,1)} %get-tuple-element.40), calls=%async_computation.2 | async-start | bytes 1572864 | tf_op jit(solution)/shard_map/all_to_all | solution.py:656

commit v4 on v3

--- a/solution.py
+++ b/solution.py
@@ -89,16 +89,24 @@
     return left, v, right
 
 
-def prep_kernel(slab_ref, x_ref, first_ref, last_ref, wide_ref, plane_ref, sem):
+def prep_kernel(slab_ref, x_ref, first_ref, last_ref, plane_ref, sem):
     channels, _, height, _ = slab_ref.shape
-    wide_ref[...] = slab_ref[:, 0].astype(F32).reshape(channels * height, 128)
-    for y in range(height):
-        v = wide_ref[pl.ds(y, channels, stride=height), :]
-        rows = slice(32 * (y % CY), 32 * (y % CY) + 32)
-        lanes = slice(128 * (y // CY), 128 * (y // CY) + 128)
-        for c, w in enumerate(shifted(v)):
-            x_ref[c, 0, rows, lanes] = w.astype(BF16)
-        plane_ref[pl.program_id(0), rows, lanes] = v.astype(BF16)
+    to = lax.broadcasted_iota(jnp.int32, (256, 256), 0)
+    source = lax.broadcasted_iota(jnp.int32, (256, 256), 1)
+    exchange = (to // 16 == source % 16) & (to % 16 == source // 16)
+    exchange = jnp.where(exchange, 1.0, 0.0).astype(BF16)
+    for h in range(channels // 16):
+        for g in range(height // 16):
+            block = slab_ref[16 * h : 16 * h + 16, 0, 16 * g : 16 * g + 16, :]
+            out = jnp.dot(exchange, block.reshape(256, 128), preferred_element_type=F32)
+            for k in range(16):
+                y = 16 * g + k
+                v = out[16 * k : 16 * k + 16]
+                rows = slice(32 * (y % CY) + 16 * h, 32 * (y % CY) + 16 * h + 16)
+                lanes = slice(128 * (y // CY), 128 * (y // CY) + 128)
+                for c, w in enumerate(shifted(v)):
+                    x_ref[c, 0, rows, lanes] = w.astype(BF16)
+                plane_ref[pl.program_id(0), rows, lanes] = v.astype(BF16)
     last = pl.num_programs(0) - 1
     first_copy = pltpu.make_async_copy(plane_ref.at[0], first_ref.at[0], sem.at[0])
     last_copy = pltpu.make_async_copy(plane_ref.at[last], last_ref.at[0], sem.at[1])
@@ -166,15 +174,11 @@
             m2_ref[...] = jnp.where(here, jnp.sum(square, axis=1, keepdims=True), m2_ref[...])
 
     convolve(0)
-
-    def step(p, _):
-        before = u_ref[pl.ds(pl.multiple_of(128 * p, 128), 128), :]
-        convolve(p + 1)
-        statistics(p, before)
-        return 0
-
     pairs = u_ref.shape[0] // 128
-    lax.fori_loop(0, pairs - 1, step, 0)
+    for p in range(1, pairs):
+        before = u_ref[128 * p - 128 : 128 * p, :]
+        convolve(p)
+        statistics(p - 1, before)
     statistics(pairs - 1, u_ref[128 * (pairs - 1) :, :])
     stat = jnp.concatenate([s1_ref[...], m2_ref[...]], axis=0).T[:16]
     low = lanes[:16] < 64
@@ -493,7 +497,7 @@
     for q in range(4):
         arrive[2 * q].wait()
         arrive[2 * q + 1].wait()
-        lax.fori_loop(4 * q, 4 * q + 4, block, 0, unroll=2)
+        lax.fori_loop(4 * q, 4 * q + 4, block, 0, unroll=4)
     for c in range(3):
         arrive[8 + c].wait()
         dt_ref[:, 256 * c : 256 * c + 256] = lax.dot_general(
@@ -574,7 +578,6 @@
             HBM,
         ),
         scratch_shapes=[
-            pltpu.VMEM((channels * height, columns), F32),
             pltpu.VMEM((planes, CY * channels, cells), BF16),
             DMA((2,)),
         ],

time: 114 us -> 112 us (0.982)
  Pallas kernels: 38.6 us -> 36.7 us
  transfers between devices with their start and end apart: 5 -> 5, of which waited for: 2 -> 2; matrix products, arithmetic and copies ran while one was open for 1% -> 1% of each run, Pallas kernels for 26% -> 25%
where the time goes in v4:
time: 112 us
  Pallas kernels  36.7 us (33%)
  starting transfers between devices  36.6 us (33%)
  waiting for transfers between devices  18.1 us (16%)
  blocking collectives  14.7 us (13%)
  between operations  4.03 us (4%)
  other arithmetic  1.61 us (1%)
    all_to_all x1, blocking collectives, per_device(): lax.all_to_all(final.reshape(roles * devices, 8, 128), ('role', 'dev'), 0...  14.7 us
    all_to_all x1, starting transfers between devices, per_device(): params = near(lax.all_to_all(rows, 'dev', 0, 0, tiled=True))  12.5 us
    all_to_all x1, waiting for transfers between devices, per_device(): gathered = lax.all_to_all(stats, 'dev', 0, 0, tiled=True)  12.3 us
    all_to_all x1, starting transfers between devices, per_device(): gathered = lax.all_to_all(stats, 'dev', 0, 0, tiled=True)  11.6 us
    pallas_call x1, Pallas kernels, per_device(): pl.pallas_call(score_kernel, out_shape=(jax.ShapeDtypeStruct((planes, cou...  11 us
    pallas_call x1, Pallas kernels, per_device(): pl.pallas_call(learner_kernel, out_shape=(pltpu.HBM((devices, SENT, 128),...  9.89 us
    all_to_all x1, starting transfers between devices, per_device(): arrived = lax.all_to_all(send, 'dev', 0, 0, tiled=True)  7 us
    pallas_call x1, Pallas kernels, per_device(): pl.pallas_call(gradient_kernel, out_shape=jax.ShapeDtypeStruct((roles * d...  6.24 us
  transfers between devices with their start and end apart: 5, of which 2 were waited for; matrix products, arithmetic and copies ran while one was open for 1% of the time, Pallas kernels for 25%

profile of v4, /device:TPU:1, one launch (start us, length us, event | category | flops | bytes accessed | tf_op | source)
XLA Modules:
  0.0 111.6 jit_solution(11115402037880719200)
XLA Ops:
  0.6 1.3 %pack.1 = bf16[64,8,128]{2,1,0:T(8,128)(2,1)} custom-call(f32[1,864]{1,0:T(1,128)} %weight_ref.1), custom_call_target="tpu_custom_call" | custom-call | tf_op jit(solution)/shard_map/pack/pallas_call | solution.py:552
  2.0 12.5 %all-to-all-start = ((bf16[64,8,128]{2,1,0:T(8,128)(2,1)}), bf16[64,8,128]{2,1,0:T(8,128)(2,1)S(1)}, u32[]{:S(2)}, u32[]{:S(2)}) async-start(bf16[64,8,128]{2,1,0:T(8,128)(2,1)} %pack.1), calls=%async_computation | async-start | bytes 262144 | tf_op jit(solution)/shard_map/all_to_all | solution.py:560
  14.4 3.3 %prep.1 = (bf16[3,2,128,2048]{3,2,1,0:T(8,128)(2,1)S(1)}, bf16[1,128,2048]{2,1,0:T(8,128)(2,1)}, bf16[1,128,2048]{2,1,0:T(8,128)(2,1)}) custom-call(bf16[32,2,64,128]{3,2,1,0:T(8,128)(2,1)} %bitcast.18), custom_call_target="tpu_custom_call" | custom-call | flops 10000000 | bytes 4194304 | tf_op jit(solution)/shard_map/prep/pallas_call | solution.py:566
  17.8 3.6 %collective-permute-start = (bf16[1,128,2048]{2,1,0:T(8,128)(2,1)}, bf16[1,128,2048]{2,1,0:T(8,128)(2,1)}, u32[]{:S(2)}, u32[]{:S(2)}) collective-permute-start(bf16[1,128,2048]{2,1,0:T(8,128)(2,1)} %get-tuple-element.27), channel_id=1, source_target_pairs={{0,1},{1,2},{2,3},{3,4},{4,5},{5,6},{6,7},{7,8},{8,9},{9,10},{10,1... | collective-permute-start | bytes 1572872 | tf_op jit(solution)/shard_map/ppermute | solution.py:622
  21.3 1.9 %collective-permute-start.1 = (bf16[1,128,2048]{2,1,0:T(8,128)(2,1)}, bf16[1,128,2048]{2,1,0:T(8,128)(2,1)}, u32[]{:S(2)}, u32[]{:S(2)}) collective-permute-start(bf16[1,128,2048]{2,1,0:T(8,128)(2,1)} %get-tuple-element.28), channel_id=1, source_target_pairs={{1,0},{2,1},{3,2},{4,3},{5,4},{6,5},{7,6},{8,7},{9,8},{10,9},{11,1... | collective-permute-start | bytes 1572872 | tf_op jit(solution)/shard_map/ppermute | solution.py:623
  26.5 0.0 all-to-all-done.w_ref
  26.5 0.0 copy-start.1
  26.5 0.0 copy-start.2
  26.5 4.2 %crop_conv.1 = (bf16[1024,1024]{1,0:T(8,128)(2,1)}, bf16[64,32,128]{2,1,0:T(8,128)(2,1)}) custom-call(f32[1]{0:T(128)S(6)} %copy.12.gain_ref, f32[1]{0:T(128)S(6)} %copy.13.shift_ref, f32[1]{0:T(128)S(6)} %copy.14.head_ref, f32[1]{0:T(128)S(6)} %copy.15.mean_ref, f32[1]{0:T(128)S(6)} %copy.16.var_ref, bf16[64,8,128]{2,1,0:T(8,128)(2,1)S(1)} %all-to-all-done.w_ref, ...), custom_call_target="tpu_custom_call" | custom-call | flops 1610612736 | bytes 8388608 | tf_op jit(solution)/shard_map/crop_conv/pallas_call | solution.py:590
  30.7 11.6 %all-to-all-start.1 = ((bf16[64,32,128]{2,1,0:T(8,128)(2,1)}), bf16[64,32,128]{2,1,0:T(8,128)(2,1)S(1)}, u32[]{:S(2)}, u32[]{:S(2)}) async-start(bf16[64,32,128]{2,1,0:T(8,128)(2,1)} %get-tuple-element.34), calls=%async_computation.1 | async-start | bytes 1048576 | tf_op jit(solution)/shard_map/all_to_all | solution.py:621
  42.4 0.6 fusion.2
  43.0 0.1 convert_reduce_fusion
  43.2 0.1 select_reduce_fusion
  43.3 0.7 pad_add_fusion.cb_ref
  44.0 12.3 %all-to-all-done.1.r_ref = bf16[64,32,128]{2,1,0:T(8,128)(2,1)S(1)} async-done(((bf16[64,32,128]{2,1,0:T(8,128)(2,1)}), bf16[64,32,128]{2,1,0:T(8,128)(2,1)S(1)}, u32[]{:S(2)}, u32[]{:S(2)}) %all-to-all-start.1) | async-done | bytes 524320 | tf_op jit(solution)/shard_map/all_to_all | solution.py:621
  56.3 9.9 %learner.1 = (bf16[64,48,128]{2,1,0:T(8,128)(2,1)}, bf16[1024,1024]{1,0:T(8,128)(2,1)}, f32[128,128]{1,0:T(8,128)S(1)}, f32[64,128]{1,0:T(8,128)S(1)}, f32[8,128...) custom-call(s32[129]{0:T(256)S(1)} %pad_add_fusion.cb_ref, ...), custom_call_target="tpu_custom_call" | custom-call | flops 10000000000 | bytes 8388608 | tf_op jit(solution)/shard_map/learner/pallas_call | solution.py:625
  66.2 7.0 %all-to-all-start.2 = ((bf16[64,48,128]{2,1,0:T(8,128)(2,1)}), bf16[64,48,128]{2,1,0:T(8,128)(2,1)S(1)}, u32[]{:S(2)}, u32[]{:S(2)}) async-start(bf16[64,48,128]{2,1,0:T(8,128)(2,1)} %get-tuple-element.40), calls=%async_computation.2 | async-start | bytes 1572864 | tf_op jit(solution)/shard_map/all_to_all | solution.py:659
  73.2 0.0 collective-permute-done.below_ref
  73.2 0.0 collective-permute-done.1.above_ref
  73.3 11.0 %score.1 = (f32[2,16,4,128]{3,2,1,0:T(4,128)}, bf16[64,3072]{1,0:T(8,128)(2,1)S(1)}) custom-call(bf16[64,8,128]{2,1,0:T(8,128)(2,1)S(1)} %all-to-all-done.w_ref, bf16[3,2,128,2048]{3,2,1,0:T(8,128)(2,1)} %copy-done, bf16[1,128,2048]{2,1,0:T(8,128)(2,1)} %collective-permute-done.below_ref, bf16[1,128,2048]{2,1,0:T(8,128)(2,1)} %collective-permute-done.1.above_ref, ...), custom_call_target="tpu_custom_call" | custom-call | flops 4831838208 | bytes 8388608 | tf_op jit(solution)/shard_map/score/pallas_call | solution.py:661
  84.3 5.7 %all-to-all-done.2 = bf16[64,48,128]{2,1,0:T(8,128)(2,1)S(1)} async-done(((bf16[64,48,128]{2,1,0:T(8,128)(2,1)}), bf16[64,48,128]{2,1,0:T(8,128)(2,1)S(1)}, u32[]{:S(2)}, u32[]{:S(2)}) %all-to-all-start.2) | async-done | bytes 786464 | tf_op jit(solution)/shard_map/all_to_all | solution.py:659
  90.0 6.2 %gradient.1 = bf16[1024,128]{1,0:T(8,128)(2,1)S(1)} custom-call(f32[64,128]{1,0:T(8,128)S(1)} %get-tuple-element.38.v_ref, bf16[3072,128]{1,0:T(8,128)(2,1)S(1)} %bitcast.12, bf16[64,3072]{1,0:T(8,128)(2,1)S(1)} %get-tuple-element.41.hot_ref, f32[128,128]{1,0:T(8,128)S(1)} %get-tuple-element.42.mr_ref, f32[8,128]{1,0:T(8,128)S(1)} %get-tuple-element.43.inv_ref, ...), custom_call_target="tpu_custom_call" | custom-call | flops 1610612736 | bytes 8388608 | tf_op jit(solution)/shard_map/gradient/pallas_call | solution.py:681
  96.2 14.7 %all_to_all.20.r_ref = bf16[128,8,128]{2,1,0:T(8,128)(2,1)S(1)} all-to-all(bf16[128,8,128]{2,1,0:T(8,128)(2,1)S(1)} %bitcast.13), channel_id=1, replica_groups=mesh['role'=2,'dev'=64] {'role','dev'}, dimensions={0} | all-to-all | bytes 524288 | tf_op jit(solution)/shard_map/all_to_all | solution.py:703
  110.9 0.7 finish.1
  (5 shorter events, 0.0 us)
Async XLA Ops:
  2.0 24.5 %all-to-all-start = ((bf16[64,8,128]{2,1,0:T(8,128)(2,1)}), bf16[64,8,128]{2,1,0:T(8,128)(2,1)S(1)}, u32[]{:S(2)}, u32[]{:S(2)}) async-start(bf16[64,8,128]{2,1,0:T(8,128)(2,1)} %pack.1), calls=%async_computation | async-start | bytes 262144 | tf_op jit(solution)/shard_map/all_to_all | solution.py:560
  17.8 13.0 %copy-start = (bf16[3,2,128,2048]{3,2,1,0:T(8,128)(2,1)}, bf16[3,2,128,2048]{3,2,1,0:T(8,128)(2,1)S(1)}, u32[]{:S(2)}) copy-start(bf16[3,2,128,2048]{3,2,1,0:T(8,128)(2,1)S(1)} %get-tuple-element.26.x_ref.x_in_ref) | copy-start | bytes 9437188
  17.8 55.5 %collective-permute-start = (bf16[1,128,2048]{2,1,0:T(8,128)(2,1)}, bf16[1,128,2048]{2,1,0:T(8,128)(2,1)}, u32[]{:S(2)}, u32[]{:S(2)}) collective-permute-start(bf16[1,128,2048]{2,1,0:T(8,128)(2,1)} %get-tuple-element.27), channel_id=1, source_target_pairs={{0,1},{1,2},{2,3},{3,4},{4,5},{5,6},{6,7},{7,8},{8,9},{9,10},{10,1... | collective-permute-start | bytes 1572872 | tf_op jit(solution)/shard_map/ppermute | solution.py:622
  21.3 51.9 %collective-permute-start.1 = (bf16[1,128,2048]{2,1,0:T(8,128)(2,1)}, bf16[1,128,2048]{2,1,0:T(8,128)(2,1)}, u32[]{:S(2)}, u32[]{:S(2)}) collective-permute-start(bf16[1,128,2048]{2,1,0:T(8,128)(2,1)} %get-tuple-element.28), channel_id=1, source_target_pairs={{1,0},{2,1},{3,2},{4,3},{5,4},{6,5},{7,6},{8,7},{9,8},{10,9},{11,1... | collective-permute-start | bytes 1572872 | tf_op jit(solution)/shard_map/ppermute | solution.py:623
  26.5 15.9 %copy-start.1 = (s32[1,64,64]{2,1,0:T(8,128)S(1)}, s32[1,64,64]{2,1,0:T(8,128)}, u32[]{:S(2)}) copy-start(s32[1,64,64]{2,1,0:T(8,128)} %param.11) | copy-start | bytes 49156
  26.5 29.8 %copy-start.2 = (bf16[1,2,64,128]{3,2,1,0:T(8,128)(2,1)S(1)}, bf16[1,2,64,128]{3,2,1,0:T(8,128)(2,1)}, u32[]{:S(2)}) copy-start(bf16[1,2,64,128]{3,2,1,0:T(8,128)(2,1)} %param.10) | copy-start | bytes 98308
  30.7 25.6 %all-to-all-start.1 = ((bf16[64,32,128]{2,1,0:T(8,128)(2,1)}), bf16[64,32,128]{2,1,0:T(8,128)(2,1)S(1)}, u32[]{:S(2)}, u32[]{:S(2)}) async-start(bf16[64,32,128]{2,1,0:T(8,128)(2,1)} %get-tuple-element.34), calls=%async_computation.1 | async-start | bytes 1048576 | tf_op jit(solution)/shard_map/all_to_all | solution.py:621
  66.2 23.8 %all-to-all-start.2 = ((bf16[64,48,128]{2,1,0:T(8,128)(2,1)}), bf16[64,48,128]{2,1,0:T(8,128)(2,1)S(1)}, u32[]{:S(2)}, u32[]{:S(2)}) async-start(bf16[64,48,128]{2,1,0:T(8,128)(2,1)} %get-tuple-element.40), calls=%async_computation.2 | async-start | bytes 1572864 | tf_op jit(solution)/shard_map/all_to_all | solution.py:659

commit v5 on v4

--- a/solution.py
+++ b/solution.py
@@ -365,7 +365,11 @@
     hd_ref[...] = head
     r0_ref[...] = jnp.zeros((64, 128), F32)
     ru_ref[...] = jnp.zeros((64, 128), F32)
-    acc_ref[...] = jnp.zeros_like(acc_ref)
+    zero = jnp.minimum(jnp.maximum(p[0:1], 0.0), 0.0)
+    zero = jnp.broadcast_to(zero, (64, 128))
+    for j in range(8):
+        for b in range(acc_ref.shape[0] // 64):
+            acc_ref[64 * b : 64 * b + 64, 128 * j : 128 * j + 128] = zero
     part_ref[...] = jnp.zeros_like(part_ref)
     live = cb_ref[2 * learners]
     arrive.wait()
@@ -425,6 +429,12 @@
         keep(e, fetch(e))
     steps = (live + 1) // 2
     lax.fori_loop(0, steps, step, 0)
+    leaves = []
+    for j in range(8):
+        rows = slice(128 * j, 128 * j + 128)
+        g_ref[rows, :] = acc_ref[rows, :].astype(BF16)
+        leaves.append(pltpu.make_async_copy(g_ref.at[rows], g_out_ref.at[rows], sem.at[2 + j]))
+        leaves[j].start()
     for e in range(2):
         reduce(2 * steps - 2 + e, e)
     r0 = r0_ref[...]
@@ -439,12 +449,6 @@
     lax.fori_loop(0, send_ref.shape[0], spread, 0, unroll=8)
     send = pltpu.make_async_copy(send_ref, send_out_ref, sem.at[1])
     send.start()
-    leaves = []
-    for j in range(8):
-        rows = slice(128 * j, 128 * j + 128)
-        g_ref[rows, :] = acc_ref[rows, :].astype(BF16)
-        leaves.append(pltpu.make_async_copy(g_ref.at[rows], g_out_ref.at[rows], sem.at[2 + j]))
-        leaves[j].start()
     dgain = jnp.sum(head * r1, axis=1, keepdims=True)
     dshift = jnp.sum(head * r0, axis=1, keepdims=True)
     dhead = jnp.sum(gain * r1 + shift * r0, axis=1, keepdims=True)

time: 112 us -> 112 us (level)
  no operation moved by 1% of the time
where the time goes in v5:
time: 112 us; the launch traced here: 111 us
  starting transfers between devices  36.6 us (33%)
  Pallas kernels  36.5 us (33%)
  waiting for transfers between devices  18.1 us (16%)
  blocking collectives  14.7 us (13%)
  between operations  4.03 us (4%)
  other arithmetic  1.61 us (1%)
    all_to_all x1, blocking collectives, per_device(): lax.all_to_all(final.reshape(roles * devices, 8, 128), ('role', 'dev'), 0...  14.7 us
    all_to_all x1, starting transfers between devices, per_device(): params = near(lax.all_to_all(rows, 'dev', 0, 0, tiled=True))  12.5 us
    all_to_all x1, waiting for transfers between devices, per_device(): gathered = lax.all_to_all(stats, 'dev', 0, 0, tiled=True)  12.3 us
    all_to_all x1, starting transfers between devices, per_device(): gathered = lax.all_to_all(stats, 'dev', 0, 0, tiled=True)  11.6 us
    pallas_call x1, Pallas kernels, per_device(): pl.pallas_call(score_kernel, out_shape=(jax.ShapeDtypeStruct((planes, cou...  11 us
    pallas_call x1, Pallas kernels, per_device(): pl.pallas_call(learner_kernel, out_shape=(pltpu.HBM((devices, SENT, 128),...  9.74 us
    all_to_all x1, starting transfers between devices, per_device(): arrived = lax.all_to_all(send, 'dev', 0, 0, tiled=True)  7 us
    pallas_call x1, Pallas kernels, per_device(): pl.pallas_call(gradient_kernel, out_shape=jax.ShapeDtypeStruct((roles * d...  6.24 us
  transfers between devices with their start and end apart: 5, of which 2 were waited for; matrix products, arithmetic and copies ran while one was open for 1% of the time, Pallas kernels for 25%

profile of v5, /device:TPU:1, one launch (start us, length us, event | category | flops | bytes accessed | tf_op | source)
XLA Modules:
  0.0 111.5 jit_solution(7231624788379937682)
XLA Ops:
  0.6 1.3 %pack.1 = bf16[64,8,128]{2,1,0:T(8,128)(2,1)} custom-call(f32[1,864]{1,0:T(1,128)} %weight_ref.1), custom_call_target="tpu_custom_call" | custom-call | tf_op jit(solution)/shard_map/pack/pallas_call | solution.py:556
  2.0 12.5 %all-to-all-start = ((bf16[64,8,128]{2,1,0:T(8,128)(2,1)}), bf16[64,8,128]{2,1,0:T(8,128)(2,1)S(1)}, u32[]{:S(2)}, u32[]{:S(2)}) async-start(bf16[64,8,128]{2,1,0:T(8,128)(2,1)} %pack.1), calls=%async_computation | async-start | bytes 262144 | tf_op jit(solution)/shard_map/all_to_all | solution.py:564
  14.4 3.3 %prep.1 = (bf16[3,2,128,2048]{3,2,1,0:T(8,128)(2,1)S(1)}, bf16[1,128,2048]{2,1,0:T(8,128)(2,1)}, bf16[1,128,2048]{2,1,0:T(8,128)(2,1)}) custom-call(bf16[32,2,64,128]{3,2,1,0:T(8,128)(2,1)} %bitcast.18), custom_call_target="tpu_custom_call" | custom-call | flops 10000000 | bytes 4194304 | tf_op jit(solution)/shard_map/prep/pallas_call | solution.py:570
  17.8 3.6 %collective-permute-start = (bf16[1,128,2048]{2,1,0:T(8,128)(2,1)}, bf16[1,128,2048]{2,1,0:T(8,128)(2,1)}, u32[]{:S(2)}, u32[]{:S(2)}) collective-permute-start(bf16[1,128,2048]{2,1,0:T(8,128)(2,1)} %get-tuple-element.27), channel_id=1, source_target_pairs={{0,1},{1,2},{2,3},{3,4},{4,5},{5,6},{6,7},{7,8},{8,9},{9,10},{10,1... | collective-permute-start | bytes 1572872 | tf_op jit(solution)/shard_map/ppermute | solution.py:626
  21.3 1.9 %collective-permute-start.1 = (bf16[1,128,2048]{2,1,0:T(8,128)(2,1)}, bf16[1,128,2048]{2,1,0:T(8,128)(2,1)}, u32[]{:S(2)}, u32[]{:S(2)}) collective-permute-start(bf16[1,128,2048]{2,1,0:T(8,128)(2,1)} %get-tuple-element.28), channel_id=1, source_target_pairs={{1,0},{2,1},{3,2},{4,3},{5,4},{6,5},{7,6},{8,7},{9,8},{10,9},{11,1... | collective-permute-start | bytes 1572872 | tf_op jit(solution)/shard_map/ppermute | solution.py:627
  26.5 0.0 all-to-all-done.w_ref
  26.5 0.0 copy-start.1
  26.5 0.0 copy-start.2
  26.5 4.2 %crop_conv.1 = (bf16[1024,1024]{1,0:T(8,128)(2,1)}, bf16[64,32,128]{2,1,0:T(8,128)(2,1)}) custom-call(f32[1]{0:T(128)S(6)} %copy.12.gain_ref, f32[1]{0:T(128)S(6)} %copy.13.shift_ref, f32[1]{0:T(128)S(6)} %copy.14.head_ref, f32[1]{0:T(128)S(6)} %copy.15.mean_ref, f32[1]{0:T(128)S(6)} %copy.16.var_ref, bf16[64,8,128]{2,1,0:T(8,128)(2,1)S(1)} %all-to-all-done.w_ref, ...), custom_call_target="tpu_custom_call" | custom-call | flops 1610612736 | bytes 8388608 | tf_op jit(solution)/shard_map/crop_conv/pallas_call | solution.py:594
  30.7 11.6 %all-to-all-start.1 = ((bf16[64,32,128]{2,1,0:T(8,128)(2,1)}), bf16[64,32,128]{2,1,0:T(8,128)(2,1)S(1)}, u32[]{:S(2)}, u32[]{:S(2)}) async-start(bf16[64,32,128]{2,1,0:T(8,128)(2,1)} %get-tuple-element.34), calls=%async_computation.1 | async-start | bytes 1048576 | tf_op jit(solution)/shard_map/all_to_all | solution.py:625
  42.4 0.6 fusion.2
  43.0 0.1 convert_reduce_fusion
  43.2 0.1 select_reduce_fusion
  43.3 0.7 pad_add_fusion.cb_ref
  44.0 12.3 %all-to-all-done.1.r_ref = bf16[64,32,128]{2,1,0:T(8,128)(2,1)S(1)} async-done(((bf16[64,32,128]{2,1,0:T(8,128)(2,1)}), bf16[64,32,128]{2,1,0:T(8,128)(2,1)S(1)}, u32[]{:S(2)}, u32[]{:S(2)}) %all-to-all-start.1) | async-done | bytes 524320 | tf_op jit(solution)/shard_map/all_to_all | solution.py:625
  56.3 9.7 %learner.1 = (bf16[64,48,128]{2,1,0:T(8,128)(2,1)}, bf16[1024,1024]{1,0:T(8,128)(2,1)}, f32[128,128]{1,0:T(8,128)S(1)}, f32[64,128]{1,0:T(8,128)S(1)}, f32[8,128...) custom-call(s32[129]{0:T(256)S(1)} %pad_add_fusion.cb_ref, ...), custom_call_target="tpu_custom_call" | custom-call | flops 10000000000 | bytes 8388608 | tf_op jit(solution)/shard_map/learner/pallas_call | solution.py:629
  66.1 7.0 %all-to-all-start.2 = ((bf16[64,48,128]{2,1,0:T(8,128)(2,1)}), bf16[64,48,128]{2,1,0:T(8,128)(2,1)S(1)}, u32[]{:S(2)}, u32[]{:S(2)}) async-start(bf16[64,48,128]{2,1,0:T(8,128)(2,1)} %get-tuple-element.40), calls=%async_computation.2 | async-start | bytes 1572864 | tf_op jit(solution)/shard_map/all_to_all | solution.py:663
  73.1 0.0 collective-permute-done.below_ref
  73.1 0.0 collective-permute-done.1.above_ref
  73.1 11.0 %score.1 = (f32[2,16,4,128]{3,2,1,0:T(4,128)}, bf16[64,3072]{1,0:T(8,128)(2,1)S(1)}) custom-call(bf16[64,8,128]{2,1,0:T(8,128)(2,1)S(1)} %all-to-all-done.w_ref, bf16[3,2,128,2048]{3,2,1,0:T(8,128)(2,1)} %copy-done, bf16[1,128,2048]{2,1,0:T(8,128)(2,1)} %collective-permute-done.below_ref, bf16[1,128,2048]{2,1,0:T(8,128)(2,1)} %collective-permute-done.1.above_ref, ...), custom_call_target="tpu_custom_call" | custom-call | flops 4831838208 | bytes 8388608 | tf_op jit(solution)/shard_map/score/pallas_call | solution.py:665
  84.1 5.7 %all-to-all-done.2 = bf16[64,48,128]{2,1,0:T(8,128)(2,1)S(1)} async-done(((bf16[64,48,128]{2,1,0:T(8,128)(2,1)}), bf16[64,48,128]{2,1,0:T(8,128)(2,1)S(1)}, u32[]{:S(2)}, u32[]{:S(2)}) %all-to-all-start.2) | async-done | bytes 786464 | tf_op jit(solution)/shard_map/all_to_all | solution.py:663
  89.8 6.2 %gradient.1 = bf16[1024,128]{1,0:T(8,128)(2,1)S(1)} custom-call(f32[64,128]{1,0:T(8,128)S(1)} %get-tuple-element.38.v_ref, bf16[3072,128]{1,0:T(8,128)(2,1)S(1)} %bitcast.12, bf16[64,3072]{1,0:T(8,128)(2,1)S(1)} %get-tuple-element.41.hot_ref, f32[128,128]{1,0:T(8,128)S(1)} %get-tuple-element.42.mr_ref, f32[8,128]{1,0:T(8,128)S(1)} %get-tuple-element.43.inv_ref, ...), custom_call_target="tpu_custom_call" | custom-call | flops 1610612736 | bytes 8388608 | tf_op jit(solution)/shard_map/gradient/pallas_call | solution.py:685
  96.1 14.7 %all_to_all.20.r_ref = bf16[128,8,128]{2,1,0:T(8,128)(2,1)S(1)} all-to-all(bf16[128,8,128]{2,1,0:T(8,128)(2,1)S(1)} %bitcast.13), channel_id=1, replica_groups=mesh['role'=2,'dev'=64] {'role','dev'}, dimensions={0} | all-to-all | bytes 524288 | tf_op jit(solution)/shard_map/all_to_all | solution.py:707
  110.8 0.7 finish.1
  (5 shorter events, 0.0 us)
Async XLA Ops:
  2.0 24.5 %all-to-all-start = ((bf16[64,8,128]{2,1,0:T(8,128)(2,1)}), bf16[64,8,128]{2,1,0:T(8,128)(2,1)S(1)}, u32[]{:S(2)}, u32[]{:S(2)}) async-start(bf16[64,8,128]{2,1,0:T(8,128)(2,1)} %pack.1), calls=%async_computation | async-start | bytes 262144 | tf_op jit(solution)/shard_map/all_to_all | solution.py:564
  17.8 13.0 %copy-start = (bf16[3,2,128,2048]{3,2,1,0:T(8,128)(2,1)}, bf16[3,2,128,2048]{3,2,1,0:T(8,128)(2,1)S(1)}, u32[]{:S(2)}) copy-start(bf16[3,2,128,2048]{3,2,1,0:T(8,128)(2,1)S(1)} %get-tuple-element.26.x_ref.x_in_ref) | copy-start | bytes 9437188
  17.8 55.3 %collective-permute-start = (bf16[1,128,2048]{2,1,0:T(8,128)(2,1)}, bf16[1,128,2048]{2,1,0:T(8,128)(2,1)}, u32[]{:S(2)}, u32[]{:S(2)}) collective-permute-start(bf16[1,128,2048]{2,1,0:T(8,128)(2,1)} %get-tuple-element.27), channel_id=1, source_target_pairs={{0,1},{1,2},{2,3},{3,4},{4,5},{5,6},{6,7},{7,8},{8,9},{9,10},{10,1... | collective-permute-start | bytes 1572872 | tf_op jit(solution)/shard_map/ppermute | solution.py:626
  21.3 51.8 %collective-permute-start.1 = (bf16[1,128,2048]{2,1,0:T(8,128)(2,1)}, bf16[1,128,2048]{2,1,0:T(8,128)(2,1)}, u32[]{:S(2)}, u32[]{:S(2)}) collective-permute-start(bf16[1,128,2048]{2,1,0:T(8,128)(2,1)} %get-tuple-element.28), channel_id=1, source_target_pairs={{1,0},{2,1},{3,2},{4,3},{5,4},{6,5},{7,6},{8,7},{9,8},{10,9},{11,1... | collective-permute-start | bytes 1572872 | tf_op jit(solution)/shard_map/ppermute | solution.py:627
  26.5 15.9 %copy-start.1 = (s32[1,64,64]{2,1,0:T(8,128)S(1)}, s32[1,64,64]{2,1,0:T(8,128)}, u32[]{:S(2)}) copy-start(s32[1,64,64]{2,1,0:T(8,128)} %param.11) | copy-start | bytes 49156
  26.5 29.8 %copy-start.2 = (bf16[1,2,64,128]{3,2,1,0:T(8,128)(2,1)S(1)}, bf16[1,2,64,128]{3,2,1,0:T(8,128)(2,1)}, u32[]{:S(2)}) copy-start(bf16[1,2,64,128]{3,2,1,0:T(8,128)(2,1)} %param.10) | copy-start | bytes 98308
  30.7 25.6 %all-to-all-start.1 = ((bf16[64,32,128]{2,1,0:T(8,128)(2,1)}), bf16[64,32,128]{2,1,0:T(8,128)(2,1)S(1)}, u32[]{:S(2)}, u32[]{:S(2)}) async-start(bf16[64,32,128]{2,1,0:T(8,128)(2,1)} %get-tuple-element.34), calls=%async_computation.1 | async-start | bytes 1048576 | tf_op jit(solution)/shard_map/all_to_all | solution.py:625
  66.1 23.8 %all-to-all-start.2 = ((bf16[64,48,128]{2,1,0:T(8,128)(2,1)}), bf16[64,48,128]{2,1,0:T(8,128)(2,1)S(1)}, u32[]{:S(2)}, u32[]{:S(2)}) async-start(bf16[64,48,128]{2,1,0:T(8,128)(2,1)} %get-tuple-element.40), calls=%async_computation.2 | async-start | bytes 1572864 | tf_op jit(solution)/shard_map/all_to_all | solution.py:663
